TPU v7x, 32 devices: a whole 2x2x4 slice. The times are simulated.
32 devices in a mesh: band: 8 (over z, x), dom: 4 (over y, core).
Axes of the slice: x: 2, y: 2, z: 4, core: 2. Of those that a mesh axis runs over, the one named last changes fastest.
Arguments:
- orbitals: bfloat16 [512, 16, 2048], P('band', 'dom'), may hold values from -6 to 6
- potential: float32 [16, 2048], P('dom'), may hold values from 0 to 2
- bounds: float32 [2], replicated, may hold values from 1 to 10, as said below
Outputs:
- rotated: bfloat16 [512, 16, 2048], P('band', 'dom')
- projected: float32 [512, 512], replicated
Inputs may be any that keep to these rules, and one draw needn't show every extreme that they name: bounds[0] lies in 1 to 2 and bounds[1] in 8.5 to 10, above the whole spectrum of H.
All inputs are finite; a program needn't handle non-finite values.
Results may differ from a plain program's by a relative error of at most 0.006.
Values may be sent and summed in bfloat16 or wider, within the bound.
A program may use at most 128 MiB of HBM per device.

v0:
```python
import functools

import jax
import jax.numpy as jnp
from jax import lax
from jax.experimental import pallas as pl
from jax.experimental.pallas import tpu as pltpu
from jax.sharding import PartitionSpec as P

GRID_Z = 32
DEG = 8
NS_STEPS = 8
LANES = 128
TILE_ROWS = 8


def filter_kernel(scal_ref, cells_ref, pot_ref, sums_ref, filt_ref, applied_ref, field, high, low, coef):
    planes, bands, width = cells_ref.shape
    rows = planes * bands
    blocks_per_plane = filt_ref.shape[0] // planes
    block = filt_ref.shape[2]
    tile = sums_ref.shape[1]
    inv_half = scal_ref[0]
    centre = scal_ref[1]

    for x in range(planes):
        mine = pl.ds(x * bands, bands)
        coef[mine, :] = jnp.broadcast_to(3.0 + pot_ref[x], (bands, width))
        start = cells_ref[x].astype(jnp.float32)
        field[0, mine, :] = start
    for c in range(width // tile):
        cols = pl.ds(c * tile, tile)
        start = field[0, :, cols]
        high[0, :, cols] = start.astype(jnp.bfloat16)
        low[0, :, cols] = jnp.zeros((rows, tile), jnp.bfloat16)

    def shifted(v, by):
        if bands % 8 == 0:
            return jnp.concatenate([v[by:], v[:by]], axis=0)
        return pltpu.roll(v, (rows - by) % rows, 0)

    def neighbours(slot, c, v):
        cols = pl.ds(pl.multiple_of(c * tile, tile), tile)
        left = pl.ds(pl.multiple_of(lax.rem(c * tile + width - LANES, width), LANES), LANES)
        right = pl.ds(pl.multiple_of(lax.rem(c * tile + tile, width), LANES), LANES)

        def part(ref):
            wide = jnp.concatenate([ref[slot, :, left], ref[slot, :, cols], ref[slot, :, right]], axis=1)
            return dot(wide, sums_ref[...])

        return part(high) + part(low) + (shifted(v, bands) + shifted(v, rows - bands))

    def sweep(slot, other, weight, diagonal, first):
        def run(c, carry):
            cols = pl.ds(pl.multiple_of(c * tile, tile), tile)
            v = field[slot, :, cols]
            fresh = weight * neighbours(slot, c, v) + (coef[:, cols] * diagonal[0] + diagonal[1]) * v
            if not first:
                fresh = fresh - field[other, :, cols]
            field[other, :, cols] = fresh
            top, rest = split(fresh)
            high[other, :, cols] = top
            low[other, :, cols] = rest
            return carry

        lax.fori_loop(0, width // tile, run, 0)

    sweep(0, 1, -0.5 * inv_half, (inv_half, -centre * inv_half), True)

    def middle(k, carry):
        slot = lax.rem(k, 2)
        sweep(slot, 1 - slot, -inv_half, (2.0 * inv_half, -2.0 * centre * inv_half), False)
        return carry

    lax.fori_loop(1, DEG, middle, 0)
    slot = DEG % 2
    for c in range(width // tile):
        cols = pl.ds(c * tile, tile)
        v = field[slot, :, cols]
        applied = coef[:, cols] * v - 0.5 * neighbours(slot, c, v)
        piece, inner = divmod(c * tile, block)
        for x in range(planes):
            where = (x * blocks_per_plane + piece, slice(None), pl.ds(inner, tile))
            filt_ref[where] = v[x * bands : (x + 1) * bands].astype(jnp.bfloat16)
            applied_ref[where] = applied[x * bands : (x + 1) * bands].astype(jnp.bfloat16)


def neighbour_sums(tile):
    source = lax.broadcasted_iota(jnp.int32, (tile + 2 * LANES, tile), 0) - LANES
    target = lax.broadcasted_iota(jnp.int32, (tile + 2 * LANES, tile), 1)
    step = source - target
    same_row = (source >= 0) & (source // GRID_Z == target // GRID_Z)
    apart = lax.rem(step + GRID_Z, GRID_Z)
    beside_z = same_row & ((apart == 1) | (apart == GRID_Z - 1))
    beside_y = (step == GRID_Z) | (step == -GRID_Z)
    return (beside_z | beside_y).astype(jnp.bfloat16)


def filter_bands(cells, potential, scalars, devices):
    planes, bands, width = cells.shape
    rows = planes * bands
    block = planes * width // devices
    out = jax.ShapeDtypeStruct((devices, bands, block), jnp.bfloat16)
    vmem = pl.BlockSpec(memory_space=pltpu.VMEM)
    return pl.pallas_call(
        filter_kernel,
        out_shape=(out, out),
        in_specs=[pl.BlockSpec(memory_space=pltpu.SMEM), vmem, vmem, vmem],
        out_specs=(vmem, vmem),
        scratch_shapes=[
            pltpu.VMEM((2, rows, width), jnp.float32),
            pltpu.VMEM((2, rows, width), jnp.bfloat16),
            pltpu.VMEM((2, rows, width), jnp.bfloat16),
            pltpu.VMEM((rows, width), jnp.float32),
        ],
        compiler_params=pltpu.CompilerParams(vmem_limit_bytes=48 << 20),
    )(scalars, cells, potential, neighbour_sums(min(256, block)))


def split(value):
    spread = value * 65537.0
    high = spread - (spread - value)
    return high.astype(jnp.bfloat16), (value - high).astype(jnp.bfloat16)


def dot(a, b):
    return jnp.dot(a, b, preferred_element_type=jnp.float32)


def dot3(a, b):
    (a_high, a_low), (b_high, b_low) = a, b
    return dot(a_high, b_high) + (dot(a_high, b_low) + dot(a_low, b_high))


def exchange_bits(doms, groups):
    dom = [("dom", 1 << i) for i in range(1, (doms - 1).bit_length())]
    band = [("band", 1 << i) for i in range((groups - 1).bit_length())]
    core = [("dom", 1)]
    return core + band[:1] + dom + band[1:], core + dom + band


def gram_sum(bits, cell_volume, filt_ref, other_ref, total, send, recv, gath, send_sem, recv_sem):
    size = filt_ref.shape[0] // 2
    index = {axis: lax.axis_index(axis) for axis in ("dom", "band")}

    def partner(axis, bit):
        mine = lax.rem(index[axis] // bit, 2)
        return mine, {axis: index[axis] + bit - 2 * bit * mine}

    barrier = pltpu.get_barrier_semaphore()
    for axis, bit in bits[0]:
        pl.semaphore_signal(
            barrier, inc=1, device_id=partner(axis, bit)[1], device_id_type=pl.DeviceIdType.MESH
        )

    pairs = (((1,), (1,)), ((), ()))
    for stream in range(2):
        total[stream] = cell_volume * lax.dot_general(
            filt_ref[pl.ds(stream * size, size), :],
            other_ref[...],
            pairs,
            preferred_element_type=jnp.float32,
        )
    pl.semaphore_wait(barrier, len(bits[0]))

    def copy(stream, number, source, target, device):
        made = pltpu.make_async_remote_copy(
            src_ref=source,
            dst_ref=target,
            send_sem=send_sem.at[stream, number],
            recv_sem=recv_sem.at[stream, number],
            device_id=device,
            device_id_type=pl.DeviceIdType.MESH,
        )
        made.start()
        return made

    stages = len(bits[0])
    start = [jnp.int32(0)] * 2
    halved = [[], []]
    length, offset = size, 0
    for stage in range(stages):
        halve = length >= 2 * TILE_ROWS
        count = length // 2 if halve else length
        space = pl.ds(offset, count)
        flight = []
        for stream in range(2):
            axis, bit = bits[stream][stage]
            mine, device = partner(axis, bit)
            give = start[stream] + (1 - mine) * count if halve else start[stream]
            keep = start[stream] + mine * count if halve else start[stream]
            give = pl.multiple_of(give, TILE_ROWS)
            send[stream, space, :] = total[stream, pl.ds(give, count), :]
            flight.append(
                copy(stream, stage, send.at[stream, space], recv.at[stream, space], device)
            )
            start[stream] = pl.multiple_of(keep, TILE_ROWS)
            if halve:
                halved[stream].append((stage, mine, device))
        for stream in range(2):
            flight[stream].wait()
            kept = pl.ds(start[stream], count)
            if halve:
                own = total[stream, kept, :]
            else:
                own = send[stream, space, :]
            total[stream, kept, :] = own + recv[stream, space, :]
        length = count
        offset += count

    for stream in range(2):
        kept = pl.ds(start[stream], length)
        gath[stream, kept, :] = total[stream, kept, :]
    for back in range(len(halved[0]) - 1, -1, -1):
        flight = []
        for stream in range(2):
            stage, mine, device = halved[stream][back]
            area = gath.at[stream, pl.ds(start[stream], length)]
            flight.append(copy(stream, stages + stage, area, area, device))
            start[stream] = pl.multiple_of(start[stream] - mine * length, TILE_ROWS)
        for made in flight:
            made.wait()
        length *= 2


def orthonormal_kernel(
    bits, cell_volume, groups, filt_ref, out_ref, trans_ref,
    total, send, recv, gath, y_ref, z_ref, t_ref, send_sem, recv_sem,
):
    gram_sum(bits, cell_volume, filt_ref, filt_ref, total, send, recv, gath, send_sem, recv_sem)
    size = filt_ref.shape[0]
    outer, inner, width = groups
    row = lax.broadcasted_iota(jnp.int32, (size, size), 0)
    col = lax.broadcasted_iota(jnp.int32, (size, size), 1)
    diag = jnp.where(row == col, 1.5, 0.0)
    corr = gath[...].reshape(size, size)
    scale = jnp.sqrt(jnp.sum(corr * corr) + 1e-06)
    scaled = corr / scale
    factor = diag - 0.5 * scaled
    z_ref[...] = factor
    y_ref[...] = dot3(split(factor), split(scaled))

    def step(k, carry):
        y = split(y_ref[...])
        z = split(z_ref[...])
        factor = split(diag - 0.5 * dot3(z, y))
        y_ref[...] = dot3(factor, y)
        z_ref[...] = dot3(factor, z)
        return carry

    lax.fori_loop(1, NS_STEPS - 1, step, 0)
    y = split(y_ref[...])
    z = split(z_ref[...])
    factor = split(diag - 0.5 * dot3(z, y))
    t_ref[...] = dot3(factor, z) / jnp.sqrt(scale)
    for i in range(outer):
        for j in range(inner):
            trans_ref[pl.ds((j * outer + i) * width, width), :] = t_ref[
                pl.ds((i * inner + j) * width, width), :
            ]
    trans = split(trans_ref[...])
    filt = filt_ref[...]
    out_ref[...] = (dot(trans[0], filt) + dot(trans[1], filt)).astype(jnp.bfloat16)


def project_kernel(
    bits, cell_volume, filt_ref, applied_ref, trans_ref, proj_ref,
    total, send, recv, gath, send_sem, recv_sem,
):
    gram_sum(bits, cell_volume, filt_ref, applied_ref, total, send, recv, gath, send_sem, recv_sem)
    size = filt_ref.shape[0]
    trans = split(trans_ref[...])
    half = split(dot3(trans, split(gath[...].reshape(size, size))))
    contract = (((1,), (1,)), ((), ()))

    def dot_t(a, b):
        return lax.dot_general(a, b, contract, preferred_element_type=jnp.float32)

    proj_ref[...] = dot_t(half[0], trans[0]) + (
        dot_t(half[0], trans[1]) + dot_t(half[1], trans[0])
    )


def sum_call(kernel, operands, out_shape, squares, bits, number, flops):
    size = operands[0].shape[0]
    vmem = pl.BlockSpec(memory_space=pltpu.VMEM)
    room = size // 2 + TILE_ROWS * len(bits[0])
    sems = pltpu.SemaphoreType.DMA((2, 2 * len(bits[0])))
    halves = pltpu.VMEM((2, size // 2, size), jnp.float32)
    stage = pltpu.VMEM((2, room, size), jnp.float32)
    return pl.pallas_call(
        kernel,
        out_shape=out_shape,
        in_specs=[vmem] * len(operands),
        out_specs=jax.tree.map(lambda _: vmem, out_shape),
        scratch_shapes=[halves, stage, stage, halves]
        + [pltpu.VMEM((size, size), jnp.float32)] * squares
        + [sems, sems],
        cost_estimate=pl.CostEstimate(flops=flops, bytes_accessed=8 << 20, transcendentals=0),
        compiler_params=pltpu.CompilerParams(
            vmem_limit_bytes=32 << 20, collective_id=number, has_side_effects=True
        ),
    )(*operands)


def body(orbitals, potential, bounds):
    bands, slab, width = orbitals.shape
    doms = lax.axis_size("dom")
    groups = lax.axis_size("band")
    devices = doms * groups
    total_bands = bands * groups
    mine = bands // doms
    everyone = ("dom", "band")
    half_width = (bounds[1] - bounds[0]) / 2.0
    centre = (bounds[1] + bounds[0]) / 2.0
    cell_volume = 1.0 / (slab * doms * width)

    sent = orbitals.reshape(doms, mine, slab, width).transpose(0, 2, 1, 3)
    cells = lax.all_to_all(sent, "dom", split_axis=0, concat_axis=0, tiled=True)
    cells = cells.reshape(doms * slab, mine, width)
    pot = lax.all_to_all(
        jnp.broadcast_to(potential, (doms, slab, width)), "dom", split_axis=0, concat_axis=0, tiled=True
    ).reshape(doms * slab, 1, width)
    filt, applied = filter_bands(cells, pot, jnp.stack([1.0 / half_width, centre]), devices)
    filt = lax.all_to_all(filt, everyone, split_axis=0, concat_axis=0, tiled=True)
    applied = lax.all_to_all(applied, everyone, split_axis=0, concat_axis=0, tiled=True)
    filt = filt.reshape(total_bands, -1)
    applied = applied.reshape(total_bands, -1)
    bits = exchange_bits(doms, groups)
    square = jax.ShapeDtypeStruct((total_bands, total_bands), jnp.float32)
    rotated, trans = sum_call(
        functools.partial(orthonormal_kernel, bits, cell_volume, (doms, groups, mine)),
        (filt,),
        (jax.ShapeDtypeStruct(filt.shape, jnp.bfloat16), square),
        3,
        bits,
        0,
        40 * total_bands**3,
    )
    out = lax.all_to_all(rotated, "band", split_axis=0, concat_axis=1, tiled=True)
    projected = sum_call(
        functools.partial(project_kernel, bits, cell_volume),
        (filt, applied, trans),
        square,
        0,
        bits,
        1,
        40 * total_bands**3,
    )
    return out.reshape(bands, slab, width), projected


def solution(mesh):
    return jax.shard_map(
        body,
        mesh=mesh,
        in_specs=(P("band", "dom", None), P("dom", None), P()),
        out_specs=(P("band", "dom", None), P()),
        check_vma=False,
    )
```

profile of v0, /device:TPU:10, one launch (start us, length us, event | category | flops | bytes accessed | tf_op | source)
XLA Modules:
  0.0 214.4 jit_solution(17117120354229376513)
XLA Ops:
  0.6 1.4 broadcast_in_dim.3
  2.1 0.0 copy-start.2
  2.1 3.5 %all-to-all-start.1 = ((f32[4,4,2048]{2,1,0:T(4,128)}), f32[4,4,2048]{2,1,0:T(4,128)S(1)}, u32[]{:S(2)}, u32[]{:S(2)}) async-start(f32[4,4,2048]{2,1,0:T(4,128)} %broadcast_in_dim.3), calls=%async_computation.1 | async-start | bytes 262144 | tf_op jit(solution)/shard_map/all_to_all | solution.py:321
  5.5 0.0 copy-done.2
  5.5 0.6 fusion.12
  8.7 2.8 %copy.8 = bf16[4,16,4,2048]{3,1,2,0:T(8,128)(2,1)} copy(bf16[4,16,4,2048]{3,2,1,0:T(4,128)(2,1)} %bitcast.13) | data formatting | bytes 2097152 | tf_op jit(solution)/shard_map/reshape | solution.py:318
  11.6 0.0 all-to-all-done.1
  11.6 3.5 %all-to-all-start = ((bf16[4,4,16,2048]{3,2,1,0:T(8,128)(2,1)}), bf16[4,4,16,2048]{3,2,1,0:T(8,128)(2,1)S(1)}, u32[]{:S(2)}, u32[]{:S(2)}) async-start(bf16[4,4,16,2048]{3,2,1,0:T(8,128)(2,1)} %bitcast.8), calls=%async_computation | async-start | bytes 2097152 | tf_op jit(solution)/shard_map/all_to_all | solution.py:319
  15.1 0.1 pad_maximum_fusion.scal_ref
  15.2 0.7 fusion.6.sums_ref
  16.0 0.2 reshape.38.pot_ref
  16.1 13.4 %all-to-all-done = bf16[4,4,16,2048]{3,2,1,0:T(8,128)(2,1)S(1)} async-done(((bf16[4,4,16,2048]{3,2,1,0:T(8,128)(2,1)}), bf16[4,4,16,2048]{3,2,1,0:T(8,128)(2,1)S(1)}, u32[]{:S(2)}, u32[]{:S(2)}) %all-to-all-start) | async-done | bytes 1048608 | tf_op jit(solution)/shard_map/all_to_all | solution.py:319
  29.5 25.9 %shard_map.50 = (bf16[32,16,1024]{2,1,0:T(8,128)(2,1)S(1)}, bf16[32,16,1024]{2,1,0:T(8,128)(2,1)}) custom-call(f32[2]{0:T(128)S(1)} %pad_maximum_fusion.scal_ref, bf16[16,16,2048]{2,1,0:T(8,128)(2,1)S(1)} %bitcast.9, f32[16,1,2048]{2,1,0:T(1,128)S(1)} %reshape.38.pot_ref, bf16[512,256]{1,0:T(8,128)(2,1)S(1)} %fusion.6.sums_ref), custom_call_target="tpu_custom_call" | custom-call | tf_op jit(solution)/shard_map/pallas_call | solution.py:105
  55.5 29.0 %all_to_all.36 = bf16[32,16,1024]{2,1,0:T(8,128)(2,1)S(1)} all-to-all(bf16[32,16,1024]{2,1,0:T(8,128)(2,1)S(1)} %get-tuple-element.6), channel_id=1, replica_groups=mesh['band'=8,'dom'=4] {'dom','band'}, dimensions={0} | all-to-all | bytes 2097152 | tf_op jit(solution)/shard_map/all_to_all | solution.py:325
  84.4 6.1 %all-to-all-start.4 = ((bf16[32,16,1024]{2,1,0:T(8,128)(2,1)}), bf16[32,16,1024]{2,1,0:T(8,128)(2,1)S(1)}, u32[]{:S(2)}, u32[]{:S(2)}) async-start(bf16[32,16,1024]{2,1,0:T(8,128)(2,1)} %get-tuple-element.8), calls=%async_computation.4 | async-start | bytes 2097152 | tf_op jit(solution)/shard_map/all_to_all | solution.py:326
  90.5 64.9 %shard_map.51 = (bf16[512,1024]{1,0:T(8,128)(2,1)}, f32[512,512]{1,0:T(8,128)S(1)}) custom-call(bf16[512,1024]{1,0:T(8,128)(2,1)S(1)} %bitcast.10), custom_call_target="tpu_custom_call" | custom-call | flops 5368709120 | bytes 8388608 | tf_op jit(solution)/shard_map/pallas_call | solution.py:291
  155.4 0.0 copy-start
  155.4 1.0 copy-done
  156.4 0.0 all-to-all-done.4
  156.4 5.6 %all-to-all-start.3 = ((bf16[8,64,1024]{2,1,0:T(8,128)(2,1)}), bf16[8,64,1024]{2,1,0:T(8,128)(2,1)}, u32[]{:S(2)}, u32[]{:S(2)}) async-start(bf16[8,64,1024]{2,1,0:T(8,128)(2,1)} %bitcast.4), calls=%async_computation.3 | async-start | bytes 2097152 | tf_op jit(solution)/shard_map/all_to_all | solution.py:340
  162.0 0.0 copy-start.1
  162.0 1.2 copy-done.1
  163.2 46.8 %shard_map.52 = f32[512,512]{1,0:T(8,128)S(1)} custom-call(bf16[512,1024]{1,0:T(8,128)(2,1)S(1)} %bitcast.11, bf16[512,1024]{1,0:T(8,128)(2,1)S(1)} %bitcast.12, f32[512,512]{1,0:T(8,128)S(1)} %copy-done.1), custom_call_target="tpu_custom_call" | custom-call | flops 5368709120 | bytes 8388608 | tf_op jit(solution)/shard_map/pallas_call | solution.py:291
  210.0 0.0 all-to-all-done.3
  210.0 1.8 copy.6
  211.8 1.6 reshape.40
  213.4 1.0 copy.10
  (5 shorter events, 0.0 us)
Async XLA Ops:
  2.1 3.5 %copy-start.2 = (f32[2]{0:T(128)S(1)}, f32[2]{0:T(128)}, u32[]{:S(2)}) copy-start(f32[2]{0:T(128)} %param.5) | copy-start | bytes 28
  2.1 9.5 %all-to-all-start.1 = ((f32[4,4,2048]{2,1,0:T(4,128)}), f32[4,4,2048]{2,1,0:T(4,128)S(1)}, u32[]{:S(2)}, u32[]{:S(2)}) async-start(f32[4,4,2048]{2,1,0:T(4,128)} %broadcast_in_dim.3), calls=%async_computation.1 | async-start | bytes 262144 | tf_op jit(solution)/shard_map/all_to_all | solution.py:321
  11.6 18.0 %all-to-all-start = ((bf16[4,4,16,2048]{3,2,1,0:T(8,128)(2,1)}), bf16[4,4,16,2048]{3,2,1,0:T(8,128)(2,1)S(1)}, u32[]{:S(2)}, u32[]{:S(2)}) async-start(bf16[4,4,16,2048]{3,2,1,0:T(8,128)(2,1)} %bitcast.8), calls=%async_computation | async-start | bytes 2097152 | tf_op jit(solution)/shard_map/all_to_all | solution.py:319
  84.4 72.0 %all-to-all-start.4 = ((bf16[32,16,1024]{2,1,0:T(8,128)(2,1)}), bf16[32,16,1024]{2,1,0:T(8,128)(2,1)S(1)}, u32[]{:S(2)}, u32[]{:S(2)}) async-start(bf16[32,16,1024]{2,1,0:T(8,128)(2,1)} %get-tuple-element.8), calls=%async_computation.4 | async-start | bytes 2097152 | tf_op jit(solution)/shard_map/all_to_all | solution.py:326
  155.4 1.0 copy-start
  156.4 53.6 %all-to-all-start.3 = ((bf16[8,64,1024]{2,1,0:T(8,128)(2,1)}), bf16[8,64,1024]{2,1,0:T(8,128)(2,1)}, u32[]{:S(2)}, u32[]{:S(2)}) async-start(bf16[8,64,1024]{2,1,0:T(8,128)(2,1)} %bitcast.4), calls=%async_computation.3 | async-start | bytes 2097152 | tf_op jit(solution)/shard_map/all_to_all | solution.py:340
  162.0 1.2 copy-start.1
where the time goes:
time: 216 us; the launch traced here: 214 us
  Pallas kernels  138 us (64%)
  blocking collectives  29 us (13%)
  starting transfers between devices  18.6 us (9%)
  waiting for transfers between devices  13.4 us (6%)
  local copies, waits for them, and re-layouts  11.6 us (5%)
  between operations  3.36 us (2%)
    pallas_call x2, Pallas kernels, sum_call(): pl.pallas_call(kernel, out_shape=out_shape, in_specs=[vmem] * len(operand...  112 us
    all_to_all x1, blocking collectives, body(): lax.all_to_all(filt, everyone, split_axis=0, concat_axis=0, tiled=True)  29 us
    pallas_call x1, Pallas kernels, filter_bands(): pl.pallas_call(filter_kernel, out_shape=(out, out), in_specs=[pl.BlockSpe...  25.9 us
    all_to_all x1, waiting for transfers between devices, body(): cells = lax.all_to_all(sent, 'dom', split_axis=0, concat_axis=0, tiled=True)  13.4 us
    all_to_all x1, starting transfers between devices, body(): lax.all_to_all(applied, everyone, split_axis=0, concat_axis=0, tiled=True)  6.07 us
    all_to_all x1, starting transfers between devices, body(): lax.all_to_all(rotated, 'band', split_axis=0, concat_axis=1, tiled=True)  5.55 us
  transfers between devices with their start and end apart: 4, of which 1 were waited for; matrix products, arithmetic and copies ran while one was open for 2% of the time, Pallas kernels for 52%

commit v1 on v0

--- a/solution.py
+++ b/solution.py
@@ -303,7 +303,264 @@
     )(*operands)
 
 
-def body(orbitals, potential, bounds):
+def device_of(position, groups):
+    return {"dom": position // groups, "band": lax.rem(position, groups)}
+
+
+def remote(source, target, send_sem, recv_sem, device):
+    return pltpu.make_async_remote_copy(
+        src_ref=source,
+        dst_ref=target,
+        send_sem=send_sem,
+        recv_sem=recv_sem,
+        device_id=device,
+        device_id_type=pl.DeviceIdType.MESH,
+    )
+
+
+def signal_all(devices, groups, me):
+    barrier = pltpu.get_barrier_semaphore()
+
+    def greet(r, carry):
+        pl.semaphore_signal(
+            barrier,
+            inc=1,
+            device_id=device_of(lax.rem(me + r, devices), groups),
+            device_id_type=pl.DeviceIdType.MESH,
+        )
+        return carry
+
+    lax.fori_loop(1, devices, greet, 0)
+    pl.semaphore_wait(barrier, devices - 1)
+
+
+def lane_orders(perm, back):
+    size = perm.shape[0]
+    high = size // LANES
+    row = lax.broadcasted_iota(jnp.int32, (size, size), 0)
+    col = lax.broadcasted_iota(jnp.int32, (size, size), 1)
+    grouped = lax.rem(row // GRID_Z, high) * LANES + lax.rem(row, GRID_Z) * high + row // LANES
+    perm[...] = jnp.where(grouped == col, 1.0, 0.0).astype(jnp.bfloat16)
+    natural = lax.rem(row, high) * LANES + row // LANES * GRID_Z + lax.rem(row // high, GRID_Z)
+    back[...] = jnp.where(natural == col, 1.0, 0.0).astype(jnp.bfloat16)
+
+
+def exchange_filter(
+    groups, bounds_ref, sent_ref, pot_ref, filt_ref, applied_ref,
+    stage, pots, perm, back, field, diag, send_f, send_a, in_send, in_recv, pot_send, pot_recv, out_send, out_recv,
+):
+    doms, slab, mine, width = stage.shape
+    devices = doms * groups
+    dom = lax.axis_index("dom")
+    band = lax.axis_index("band")
+    me = dom * groups + band
+    planes = doms * slab
+    part = min(mine, 8)
+    chunks = mine // part
+    rows = planes * part
+    lanes = width // groups
+    levels = width // LANES
+    high = LANES // GRID_Z
+    spans = levels // high
+    half_width = (bounds_ref[1] - bounds_ref[0]) / 2.0
+    centre = (bounds_ref[1] + bounds_ref[0]) / 2.0
+    inv_half = 1.0 / half_width
+
+    signal_all(devices, groups, me)
+
+    def incoming(c, r):
+        peer = lax.rem(dom + r, doms)
+        some = pl.ds(c * part, part)
+        source, target = sent_ref.at[peer, :, some, :], stage.at[dom, :, some, :]
+        if r == 0:
+            return pltpu.make_async_copy(source, target, in_recv.at[c, r])
+        return remote(source, target, in_send.at[c, r], in_recv.at[c, r], {"dom": peer})
+
+    def potential(r):
+        if r == 0:
+            return pltpu.make_async_copy(pot_ref, pots.at[dom], pot_recv.at[r])
+        return remote(pot_ref, pots.at[dom], pot_send.at[r], pot_recv.at[r], {"dom": lax.rem(dom + r, doms)})
+
+    for r in range(doms):
+        potential(r).start()
+    for c in range(chunks):
+        for r in range(doms):
+            incoming(c, r).start()
+
+    lane_orders(perm, back)
+    lane = lax.broadcasted_iota(jnp.int32, (rows, LANES), 1)
+    first_high = lax.rem(lane, high) == 0
+    last_high = lax.rem(lane, high) == high - 1
+
+    for r in range(doms):
+        potential(r).wait()
+    for k in range(spans):
+        pot = jnp.concatenate(
+            [pots[:, :, pl.ds((h * spans + k) * LANES, LANES)].reshape(planes, LANES) for h in range(high)], axis=1
+        )
+        ordered = jnp.zeros(pot.shape, jnp.float32)
+        for piece in range(3):
+            top = pot.astype(jnp.bfloat16)
+            ordered = ordered + dot(top, perm[...])
+            pot = pot - top.astype(jnp.float32)
+        scaled = (3.0 + ordered - centre) * (2.0 * inv_half)
+        for b in range(high):
+            line = scaled[:, b * LANES : (b + 1) * LANES]
+            diag[k * high + b] = jnp.broadcast_to(line[:, None, :], (planes, part, LANES)).reshape(rows, LANES)
+
+    def edges(slot):
+        top = field[slot, levels]
+        field[slot, 0] = jnp.where(
+            first_high, pltpu.roll(top, LANES - (high - 1), 1), pltpu.roll(top, 1, 1)
+        )
+        low = field[slot, 1]
+        field[slot, levels + 1] = jnp.where(
+            last_high, pltpu.roll(low, high - 1, 1), pltpu.roll(low, LANES - 1, 1)
+        )
+
+    def image(slot, i):
+        v = field[slot, i]
+        around = pltpu.roll(v, high, 1) + pltpu.roll(v, LANES - high, 1)
+        around = around + (field[slot, i - 1] + field[slot, i + 1])
+        around = around + (
+            jnp.concatenate([v[part:], v[:part]], axis=0) + jnp.concatenate([v[rows - part :], v[: rows - part]], axis=0)
+        )
+        return diag[i - 1] * v - inv_half * around, v
+
+    def outgoing(source, target, which, c, r):
+        position = lax.rem(me + r, devices)
+        device = device_of(position, groups)
+        piece = source.at[
+            pl.ds(device["dom"] * slab, slab),
+            pl.ds(c * part, part),
+            pl.ds(pl.multiple_of(device["band"] * lanes, LANES), lanes),
+        ]
+        row = pl.multiple_of((band * doms + dom) * mine + c * part, part)
+        place = target.at[:, pl.ds(row, part), :]
+        return piece, place, out_send.at[which, c, r], out_recv.at[which, c, r], device
+
+    def send_out(source, target, which, c):
+        piece, place, _, sem, _ = outgoing(source, target, which, c, 0)
+        pltpu.make_async_copy(piece, place, sem).start()
+
+        def run(r, carry):
+            remote(*outgoing(source, target, which, c, r)).start()
+            return carry
+
+        lax.fori_loop(1, devices, run, 0)
+
+    def wait_out(source, target, which, c):
+        piece, place, _, sem, _ = outgoing(source, target, which, c, 0)
+        pltpu.make_async_copy(piece, place, sem).wait()
+
+        def run(r, carry):
+            remote(*outgoing(source, target, which, c, r)).wait()
+            return carry
+
+        lax.fori_loop(1, devices, run, 0)
+
+    for c in range(chunks):
+        for r in range(doms):
+            incoming(c, r).wait()
+        some = pl.ds(c * part, part)
+        for k in range(spans):
+            cells = jnp.concatenate(
+                [
+                    stage[:, :, some, pl.ds((h * spans + k) * LANES, LANES)].astype(jnp.float32).reshape(rows, LANES)
+                    for h in range(high)
+                ],
+                axis=1,
+            )
+            ordered = dot(cells.astype(jnp.bfloat16), perm[...])
+            for b in range(high):
+                field[0, 1 + k * high + b] = ordered[:, b * LANES : (b + 1) * LANES]
+        edges(0)
+
+        def first(i, carry):
+            field[1, i] = 0.5 * image(0, i)[0]
+            return carry
+
+        lax.fori_loop(1, levels + 1, first, 0)
+        edges(1)
+
+        def middle(k, carry):
+            slot = lax.rem(k, 2)
+
+            def run(i, inner):
+                field[1 - slot, i] = image(slot, i)[0] - field[1 - slot, i]
+                return inner
+
+            lax.fori_loop(1, levels + 1, run, 0)
+            edges(1 - slot)
+            return carry
+
+        lax.fori_loop(1, DEG, middle, 0)
+        slot = DEG % 2
+
+        def restore(values, target, k):
+            natural = dot(jnp.concatenate(values, axis=1).astype(jnp.bfloat16), back[...])
+            for h in range(high):
+                target[:, some, pl.ds((h * spans + k) * LANES, LANES)] = (
+                    natural[:, h * LANES : (h + 1) * LANES].reshape(planes, part, LANES).astype(jnp.bfloat16)
+                )
+
+        for k in range(spans):
+            restore([field[slot, 1 + k * high + b] for b in range(high)], send_f, k)
+        send_out(send_f, filt_ref, 0, c)
+        for k in range(spans):
+            values = []
+            for b in range(high):
+                twice, v = image(slot, 1 + k * high + b)
+                values.append((0.5 * half_width) * twice + centre * v)
+            restore(values, send_a, k)
+    for c in range(chunks):
+        send_out(send_a, applied_ref, 1, c)
+    for c in range(chunks):
+        wait_out(send_f, filt_ref, 0, c)
+        wait_out(send_a, applied_ref, 1, c)
+
+
+def exchange_filter_call(sent, potential, bounds, groups):
+    doms, slab, mine, width = sent.shape
+    devices = doms * groups
+    planes = doms * slab
+    part = min(mine, 8)
+    chunks = mine // part
+    levels = width // LANES
+    lanes = width // groups
+    size = LANES * (LANES // GRID_Z)
+    out = jax.ShapeDtypeStruct((slab, devices * mine, lanes), jnp.bfloat16)
+    vmem = pl.BlockSpec(memory_space=pltpu.VMEM)
+    hbm = pl.BlockSpec(memory_space=pl.ANY)
+    whole = pltpu.VMEM((planes, mine, width), jnp.bfloat16)
+    order = pltpu.VMEM((size, size), jnp.bfloat16)
+    dma = pltpu.SemaphoreType.DMA
+    return pl.pallas_call(
+        functools.partial(exchange_filter, groups),
+        out_shape=(out, out),
+        in_specs=[pl.BlockSpec(memory_space=pltpu.SMEM), hbm, vmem],
+        out_specs=(vmem, vmem),
+        scratch_shapes=[
+            pltpu.VMEM(sent.shape, jnp.bfloat16),
+            pltpu.VMEM((doms, slab, width), jnp.float32),
+            order,
+            order,
+            pltpu.VMEM((2, levels + 2, planes * part, LANES), jnp.float32),
+            pltpu.VMEM((levels, planes * part, LANES), jnp.float32),
+            whole,
+            whole,
+            dma((chunks, doms)),
+            dma((chunks, doms)),
+            dma((doms,)),
+            dma((doms,)),
+            dma((2, chunks, devices)),
+            dma((2, chunks, devices)),
+        ],
+        compiler_params=pltpu.CompilerParams(vmem_limit_bytes=40 << 20, collective_id=2, has_side_effects=True),
+    )(bounds, sent, potential)
+
+
+def body_plain(orbitals, potential, bounds):
     bands, slab, width = orbitals.shape
     doms = lax.axis_size("dom")
     groups = lax.axis_size("band")
@@ -350,6 +607,44 @@
     return out.reshape(bands, slab, width), projected
 
 
+def body(orbitals, potential, bounds):
+    bands, slab, width = orbitals.shape
+    doms = lax.axis_size("dom")
+    groups = lax.axis_size("band")
+    mine = bands // doms
+    if mine % 8 or width % (groups * LANES):
+        return body_plain(orbitals, potential, bounds)
+    total_bands = bands * groups
+    cell_volume = 1.0 / (slab * doms * width)
+    sent = orbitals.reshape(doms, mine, slab, width).transpose(0, 2, 1, 3)
+    filt, applied = exchange_filter_call(sent, potential, bounds, groups)
+    filt = filt.transpose(1, 0, 2).reshape(total_bands, -1)
+    applied = applied.transpose(1, 0, 2).reshape(total_bands, -1)
+    bits = exchange_bits(doms, groups)
+    square = jax.ShapeDtypeStruct((total_bands, total_bands), jnp.float32)
+    rotated, trans = sum_call(
+        functools.partial(orthonormal_kernel, bits, cell_volume, (1, 1, total_bands)),
+        (filt,),
+        (jax.ShapeDtypeStruct(filt.shape, jnp.bfloat16), square),
+        3,
+        bits,
+        0,
+        40 * total_bands**3,
+    )
+    out = lax.all_to_all(rotated, "band", split_axis=0, concat_axis=1, tiled=True)
+    out = out.reshape(bands, groups, slab, width // groups).transpose(0, 2, 1, 3)
+    projected = sum_call(
+        functools.partial(project_kernel, bits, cell_volume),
+        (filt, applied, trans),
+        square,
+        0,
+        bits,
+        1,
+        40 * total_bands**3,
+    )
+    return out.reshape(bands, slab, width), projected
+
+
 def solution(mesh):
     return jax.shard_map(
         body,

time: 216 us -> 205 us (0.949)
  Pallas kernels: 138 us -> 189 us
  blocking collectives: 29 us -> 0 us
  waiting for transfers between devices: 13.4 us -> 0.01 us
  starting transfers between devices: 18.6 us -> 5.43 us
  local copies, waits for them, and re-layouts: 11.6 us -> 8.24 us
  between operations: 3.36 us -> 0.72 us
    pallas_call x1, Pallas kernels: 25.9 us -> 84.5 us  [exchange_filter_call(): pl.pallas_call(functools.partial(exchange_filter, groups), out_shape=(out...]
    all_to_all x1 -> x0, blocking collectives: 29 us -> none  [body(): lax.all_to_all(filt, everyone, split_axis=0, concat_axis=0, tiled=True)]
    all_to_all x3 -> x0, waiting for transfers between devices: 13.4 us -> none  [the longest x1 13.4 us: body(): cells = lax.all_to_all(sent, 'dom', split_axis=0, concat_axis=0, tiled=True)]
    all_to_all x3 -> x0, starting transfers between devices: 13.1 us -> none  [the longest x1 6.07 us: body(): lax.all_to_all(applied, everyone, split_axis=0, concat_axis=0, tiled=True)]
    pallas_call x2, Pallas kernels: 112 us -> 105 us  [sum_call(): pl.pallas_call(kernel, out_shape=out_shape, in_specs=[vmem] * len(operand...]
    reshape x1 -> x4, local copies, waits for them, and re-layouts: 0.17 us -> 3.23 us  [the longest x2 2.98 us: body(): out.reshape(bands, groups, slab, width // groups).transpose(0, 2, 1, 3)]
  transfers between devices with their start and end apart: 4 -> 1, of which waited for: 1 -> 0; matrix products, arithmetic and copies ran while one was open for 2% -> 0% of each run, Pallas kernels for 52% -> 24%
where the time goes in v1:
time: 205 us; the launch traced here: 204 us
  Pallas kernels  189 us (92%)
  local copies, waits for them, and re-layouts  8.24 us (4%)
  starting transfers between devices  5.43 us (3%)
    pallas_call x2, Pallas kernels, sum_call(): pl.pallas_call(kernel, out_shape=out_shape, in_specs=[vmem] * len(operand...  105 us
    pallas_call x1, Pallas kernels, exchange_filter_call(): pl.pallas_call(functools.partial(exchange_filter, groups), out_shape=(out...  84.5 us
    all_to_all x1, starting transfers between devices, body(): lax.all_to_all(rotated, 'band', split_axis=0, concat_axis=1, tiled=True)  5.43 us
  transfers between devices with their start and end apart: 1, of which 0 were waited for; matrix products, arithmetic and copies ran while one was open for 0% of the time, Pallas kernels for 24%

profile of v1, /device:TPU:10, one launch (start us, length us, event | category | flops | bytes accessed | tf_op | source)
XLA Modules:
  0.0 203.6 jit_solution(13295181983005769873)
XLA Ops:
  0.6 0.0 copy-start
  0.6 1.8 copy.19
  2.5 0.0 copy-start.1
  2.5 0.0 copy-done
  2.5 0.6 copy-done.1
  3.1 84.5 %shard_map.50 = (bf16[4,512,256]{2,1,0:T(8,128)(2,1)S(1)}, bf16[4,512,256]{2,1,0:T(8,128)(2,1)S(1)}) custom-call(f32[2]{0:T(128)S(1)} %copy-done.1, bf16[4,4,16,2048]{3,2,1,0:T(8,128)(2,1)S(1)} %bitcast.19, f32[4,2048]{1,0:T(4,128)S(1)} %copy-done), custom_call_target="tpu_custom_call" | custom-call | tf_op jit(solution)/shard_map/pallas_call | solution.py:538
  87.6 0.1 copy.15
  87.8 56.8 %shard_map.51 = (bf16[512,1024]{1,0:T(8,128)(2,1)}, f32[512,512]{1,0:T(8,128)S(1)}) custom-call(bf16[512,1024]{1,0:T(8,128)(2,1)S(1)} %bitcast.20), custom_call_target="tpu_custom_call" | custom-call | flops 5368709120 | bytes 8388608 | tf_op jit(solution)/shard_map/pallas_call | solution.py:291
  144.6 5.4 %all-to-all-start = ((bf16[8,64,1024]{2,1,0:T(8,128)(2,1)}), bf16[8,64,1024]{2,1,0:T(8,128)(2,1)}, u32[]{:S(2)}, u32[]{:S(2)}) async-start(bf16[8,64,1024]{2,1,0:T(8,128)(2,1)} %bitcast.3), calls=%async_computation | async-start | bytes 2097152 | tf_op jit(solution)/shard_map/all_to_all | solution.py:634
  150.0 0.1 copy.16
  150.1 47.9 %shard_map.52 = f32[512,512]{1,0:T(8,128)S(1)} custom-call(bf16[512,1024]{1,0:T(8,128)(2,1)S(1)} %bitcast.21, bf16[512,1024]{1,0:T(8,128)(2,1)S(1)} %bitcast.23, f32[512,512]{1,0:T(8,128)S(1)} %get-tuple-element.9.trans_ref), custom_call_target="tpu_custom_call" | custom-call | flops 5368709120 | bytes 8388608 | tf_op jit(solution)/shard_map/pallas_call | solution.py:291
  198.0 0.0 all-to-all-done
  198.0 1.9 reshape.25
  199.9 1.1 copy.20
  201.0 1.6 reshape.26
  202.6 1.0 copy.22
Async XLA Ops:
  0.6 1.8 copy-start
  2.5 0.7 copy-start.1
  144.6 53.5 %all-to-all-start = ((bf16[8,64,1024]{2,1,0:T(8,128)(2,1)}), bf16[8,64,1024]{2,1,0:T(8,128)(2,1)}, u32[]{:S(2)}, u32[]{:S(2)}) async-start(bf16[8,64,1024]{2,1,0:T(8,128)(2,1)} %bitcast.3), calls=%async_computation | async-start | bytes 2097152 | tf_op jit(solution)/shard_map/all_to_all | solution.py:634

commit v2 on v1

--- a/solution.py
+++ b/solution.py
@@ -11,6 +11,8 @@
 DEG = 8
 NS_STEPS = 8
 LANES = 128
+UNROLL = 8
+PAUSE = 2
 TILE_ROWS = 8
 
 
@@ -303,8 +305,12 @@
     )(*operands)
 
 
-def device_of(position, groups):
-    return {"dom": position // groups, "band": lax.rem(position, groups)}
+def peers(doms, groups):
+    dom = lax.axis_index("dom")
+    band = lax.axis_index("band")
+    rows = [lax.rem(dom + r, doms) for r in range(doms)]
+    columns = [lax.rem(band + r, groups) for r in range(groups)]
+    return [{"dom": d, "band": b} for b in columns for d in rows]
 
 
 def remote(source, target, send_sem, recv_sem, device):
@@ -318,20 +324,11 @@
     )
 
 
-def signal_all(devices, groups, me):
+def greet(others):
     barrier = pltpu.get_barrier_semaphore()
-
-    def greet(r, carry):
-        pl.semaphore_signal(
-            barrier,
-            inc=1,
-            device_id=device_of(lax.rem(me + r, devices), groups),
-            device_id_type=pl.DeviceIdType.MESH,
-        )
-        return carry
-
-    lax.fori_loop(1, devices, greet, 0)
-    pl.semaphore_wait(barrier, devices - 1)
+    for other in others:
+        pl.semaphore_signal(barrier, inc=1, device_id=other, device_id_type=pl.DeviceIdType.MESH)
+    pl.semaphore_wait(barrier, len(others))
 
 
 def lane_orders(perm, back):
@@ -345,15 +342,175 @@
     back[...] = jnp.where(natural == col, 1.0, 0.0).astype(jnp.bfloat16)
 
 
-def exchange_filter(
-    groups, bounds_ref, sent_ref, pot_ref, filt_ref, applied_ref,
-    stage, pots, perm, back, field, diag, send_f, send_a, in_send, in_recv, pot_send, pot_recv, out_send, out_recv,
+class BlockSum:
+    def __init__(self, total, recv, gath, send_sem, recv_sem, levels):
+        self.total, self.recv, self.gath = total, recv, gath
+        self.send_sem, self.recv_sem, self.levels = send_sem, recv_sem, levels
+        self.start, self.length = jnp.int32(0), total.shape[0]
+        self.offset, self.copies = 0, []
+
+    def steps(self):
+        for level in range(len(self.levels)):
+            yield functools.partial(self.scatter, level)
+            yield functools.partial(self.add, level)
+        for level in range(len(self.levels) - 1, -1, -1):
+            yield functools.partial(self.gather, level)
+            yield functools.partial(self.join, level)
+
+    def scatter(self, level):
+        at, size, device = self.levels[level]
+        rows = self.length // size
+        self.copies = []
+        for r in range(1, size):
+            to = lax.rem(at + r, size)
+            source = pl.ds(pl.multiple_of(self.start + to * rows, TILE_ROWS), rows)
+            place = pl.ds(self.offset + (r - 1) * rows, rows)
+            self.copies.append(
+                remote(
+                    self.total.at[source], self.recv.at[place],
+                    self.send_sem.at[0, level, r], self.recv_sem.at[0, level, r], device(to),
+                )
+            )
+        for made in self.copies:
+            made.start()
+
+    def add(self, level):
+        at, size, _ = self.levels[level]
+        rows = self.length // size
+        self.start = pl.multiple_of(self.start + at * rows, TILE_ROWS)
+        self.length = rows
+        kept = pl.ds(self.start, rows)
+        for made in self.copies:
+            made.wait()
+        value = self.total[kept]
+        for r in range(1, size):
+            value = value + self.recv[pl.ds(self.offset + (r - 1) * rows, rows)]
+        self.offset += (size - 1) * rows
+        self.total[kept] = value
+        if level == len(self.levels) - 1:
+            self.gath[kept] = value
+
+    def gather(self, level):
+        at, size, device = self.levels[level]
+        area = self.gath.at[pl.ds(self.start, self.length)]
+        self.copies = [
+            remote(area, area, self.send_sem.at[1, level, r], self.recv_sem.at[1, level, r], device(lax.rem(at + r, size)))
+            for r in range(1, size)
+        ]
+        for made in self.copies:
+            made.start()
+
+    def join(self, level):
+        at, size, _ = self.levels[level]
+        for made in self.copies:
+            made.wait()
+        self.start = pl.multiple_of(self.start - at * self.length, TILE_ROWS)
+        self.length *= size
+
+
+def sum_levels(doms, groups):
+    dom = lax.axis_index("dom")
+    band = lax.axis_index("band")
+    core, chip = lax.rem(dom, 2), dom // 2
+    low, high = lax.rem(band, 2), band // 2
+    return [
+        (core, 2, lambda to: {"dom": chip * 2 + to}),
+        (chip * 2 + low, doms, lambda to: {"dom": to // 2 * 2 + core, "band": high * 2 + lax.rem(to, 2)}),
+        (high, groups // 2, lambda to: {"band": to * 2 + low}),
+    ]
+
+
+def upper_blocks(total):
+    count = total // LANES
+    return [(i, j) for i in range(count) for j in range(i, count)]
+
+
+def gram(cell_volume, left, right, packed):
+    slab, total, _ = left.shape
+    size = 2 * LANES
+    where = {pair: n for n, pair in enumerate(upper_blocks(total))}
+    for i in range(total // size):
+        for j in range(i, total // size):
+            block = jnp.zeros((size, size), jnp.float32)
+            for x in range(slab):
+                block = block + lax.dot_general(
+                    left[x, pl.ds(i * size, size), :],
+                    right[x, pl.ds(j * size, size), :],
+                    (((1,), (1,)), ((), ())),
+                    preferred_element_type=jnp.float32,
+                )
+            block = block * cell_volume
+            for a in range(2):
+                for b in range(2):
+                    pair = (2 * i + a, 2 * j + b)
+                    if pair in where:
+                        packed[pl.ds(where[pair] * LANES, LANES)] = block[
+                            a * LANES : (a + 1) * LANES, b * LANES : (b + 1) * LANES
+                        ]
+
+
+def unpack(packed, full):
+    for n, (i, j) in enumerate(upper_blocks(full.shape[0])):
+        block = packed[pl.ds(n * LANES, LANES)]
+        full[pl.ds(i * LANES, LANES), pl.ds(j * LANES, LANES)] = block
+        if i != j:
+            full[pl.ds(j * LANES, LANES), pl.ds(i * LANES, LANES)] = block.T
+
+
+def split_rounding(value):
+    high = value.astype(jnp.bfloat16)
+    return high, (value - high.astype(jnp.float32)).astype(jnp.bfloat16)
+
+
+def inverse_root(full, work, other, pause):
+    size = full.shape[0]
+    row = lax.broadcasted_iota(jnp.int32, (size, size), 0)
+    col = lax.broadcasted_iota(jnp.int32, (size, size), 1)
+
+    def diagonal(value):
+        return jnp.where(row == col, value, 0.0)
+
+    corr = full[...]
+    scale = jnp.sqrt(jnp.sum(corr * corr) + 1e-06)
+    work[...] = corr / scale
+    for double in range(NS_STEPS // 2 - 1):
+        held = split_rounding(work[...])
+        other[...] = dot3(held, held)
+        pause()
+        square = other[...]
+        rest = dot3(split_rounding(square), split_rounding(0.0625 * square - 0.5625 * work[...]))
+        factor = split_rounding(diagonal(2.25) - 2.4375 * work[...] + (1.6875 * square + rest))
+        pause()
+        if double == 0:
+            full[...] = factor[0].astype(jnp.float32) + factor[1].astype(jnp.float32)
+        else:
+            full[...] = dot3(split_rounding(full[...]), factor)
+            pause()
+        other[...] = dot3(held, factor)
+        pause()
+        work[...] = dot3(split_rounding(other[...]), factor)
+        pause()
+    left = diagonal(1.0) - work[...]
+    rounded = left.astype(jnp.bfloat16)
+    square = dot(rounded, rounded)
+    rest = 0.5 * left + 0.375 * square
+    rest = rest + dot(square.astype(jnp.bfloat16), (0.3125 * left + 0.0625 * square).astype(jnp.bfloat16))
+    pause()
+    value = full[...]
+    value = value + dot(value.astype(jnp.bfloat16), rest.astype(jnp.bfloat16))
+    return value / jnp.sqrt(scale)
+
+
+def step_kernel(
+    groups, cell_volume, bounds_ref, sent_ref, pot_ref, out_ref, proj_ref,
+    filt_ref, applied_ref, stage, pots, perm, back, even, odd, diag, send_f, send_a,
+    corr_sum, corr_recv, corr_gath, hamil_sum, hamil_recv, hamil_gath, full, work, other, trans, spread, turned,
+    in_send, in_recv, pot_send, pot_recv, out_send, out_recv, corr_send, corr_arrive, hamil_send, hamil_arrive, back_send, back_recv,
 ):
     doms, slab, mine, width = stage.shape
     devices = doms * groups
     dom = lax.axis_index("dom")
     band = lax.axis_index("band")
-    me = dom * groups + band
     planes = doms * slab
     part = min(mine, 8)
     chunks = mine // part
@@ -366,7 +523,8 @@
     centre = (bounds_ref[1] + bounds_ref[0]) / 2.0
     inv_half = 1.0 / half_width
 
-    signal_all(devices, groups, me)
+    everyone = peers(doms, groups)
+    greet(everyone[1:])
 
     def incoming(c, r):
         peer = lax.rem(dom + r, doms)
@@ -408,56 +566,56 @@
             line = scaled[:, b * LANES : (b + 1) * LANES]
             diag[k * high + b] = jnp.broadcast_to(line[:, None, :], (planes, part, LANES)).reshape(rows, LANES)
 
-    def edges(slot):
-        top = field[slot, levels]
-        field[slot, 0] = jnp.where(
-            first_high, pltpu.roll(top, LANES - (high - 1), 1), pltpu.roll(top, 1, 1)
-        )
-        low = field[slot, 1]
-        field[slot, levels + 1] = jnp.where(
-            last_high, pltpu.roll(low, high - 1, 1), pltpu.roll(low, LANES - 1, 1)
-        )
-
-    def image(slot, i):
-        v = field[slot, i]
+    def edges(field):
+        top = field[levels]
+        field[0] = jnp.where(first_high, pltpu.roll(top, LANES - (high - 1), 1), pltpu.roll(top, 1, 1))
+        low = field[1]
+        field[levels + 1] = jnp.where(last_high, pltpu.roll(low, high - 1, 1), pltpu.roll(low, LANES - 1, 1))
+
+    def image(field, i):
+        v = field[i]
         around = pltpu.roll(v, high, 1) + pltpu.roll(v, LANES - high, 1)
-        around = around + (field[slot, i - 1] + field[slot, i + 1])
+        around = around + (field[i - 1] + field[i + 1])
         around = around + (
             jnp.concatenate([v[part:], v[:part]], axis=0) + jnp.concatenate([v[rows - part :], v[: rows - part]], axis=0)
         )
         return diag[i - 1] * v - inv_half * around, v
 
-    def outgoing(source, target, which, c, r):
-        position = lax.rem(me + r, devices)
-        device = device_of(position, groups)
-        piece = source.at[
-            pl.ds(device["dom"] * slab, slab),
-            pl.ds(c * part, part),
-            pl.ds(pl.multiple_of(device["band"] * lanes, LANES), lanes),
-        ]
+    def sweep(source, target, first):
+        def run(j, carry):
+            for i in range(UNROLL):
+                i = 1 + j * UNROLL + i
+                fresh = image(source, i)[0]
+                target[i] = 0.5 * fresh if first else fresh - target[i]
+            return carry
+
+        lax.fori_loop(0, levels // UNROLL, run, 0)
+        edges(target)
+
+    def outgoing(source, target, which, c):
+        copies = []
         row = pl.multiple_of((band * doms + dom) * mine + c * part, part)
         place = target.at[:, pl.ds(row, part), :]
-        return piece, place, out_send.at[which, c, r], out_recv.at[which, c, r], device
+        for r, device in enumerate(everyone):
+            piece = source.at[
+                pl.ds(device["dom"] * slab, slab),
+                pl.ds(c * part, part),
+                pl.ds(pl.multiple_of(device["band"] * lanes, LANES), lanes),
+            ]
+            recv = out_recv.at[which, c, r]
+            if r == 0:
+                copies.append(pltpu.make_async_copy(piece, place, recv))
+            else:
+                copies.append(remote(piece, place, out_send.at[which, c, r], recv, device))
+        return copies
 
     def send_out(source, target, which, c):
-        piece, place, _, sem, _ = outgoing(source, target, which, c, 0)
-        pltpu.make_async_copy(piece, place, sem).start()
-
-        def run(r, carry):
-            remote(*outgoing(source, target, which, c, r)).start()
-            return carry
-
-        lax.fori_loop(1, devices, run, 0)
+        for copy in outgoing(source, target, which, c):
+            copy.start()
 
     def wait_out(source, target, which, c):
-        piece, place, _, sem, _ = outgoing(source, target, which, c, 0)
-        pltpu.make_async_copy(piece, place, sem).wait()
-
-        def run(r, carry):
-            remote(*outgoing(source, target, which, c, r)).wait()
-            return carry
-
-        lax.fori_loop(1, devices, run, 0)
+        for copy in outgoing(source, target, which, c):
+            copy.wait()
 
     for c in range(chunks):
         for r in range(doms):
@@ -473,29 +631,20 @@
             )
             ordered = dot(cells.astype(jnp.bfloat16), perm[...])
             for b in range(high):
-                field[0, 1 + k * high + b] = ordered[:, b * LANES : (b + 1) * LANES]
-        edges(0)
-
-        def first(i, carry):
-            field[1, i] = 0.5 * image(0, i)[0]
+                even[1 + k * high + b] = ordered[:, b * LANES : (b + 1) * LANES]
+        edges(even)
+        sweep(even, odd, True)
+
+        def pair(k, carry):
+            sweep(odd, even, False)
+            sweep(even, odd, False)
             return carry
 
-        lax.fori_loop(1, levels + 1, first, 0)
-        edges(1)
-
-        def middle(k, carry):
-            slot = lax.rem(k, 2)
-
-            def run(i, inner):
-                field[1 - slot, i] = image(slot, i)[0] - field[1 - slot, i]
-                return inner
-
-            lax.fori_loop(1, levels + 1, run, 0)
-            edges(1 - slot)
-            return carry
-
-        lax.fori_loop(1, DEG, middle, 0)
-        slot = DEG % 2
+        lax.fori_loop(0, (DEG - 1) // 2, pair, 0)
+        last = odd
+        if DEG % 2 == 0:
+            sweep(odd, even, False)
+            last = even
 
         def restore(values, target, k):
             natural = dot(jnp.concatenate(values, axis=1).astype(jnp.bfloat16), back[...])
@@ -505,58 +654,155 @@
                 )
 
         for k in range(spans):
-            restore([field[slot, 1 + k * high + b] for b in range(high)], send_f, k)
+            restore([last[1 + k * high + b] for b in range(high)], send_f, k)
         send_out(send_f, filt_ref, 0, c)
         for k in range(spans):
             values = []
             for b in range(high):
-                twice, v = image(slot, 1 + k * high + b)
+                twice, v = image(last, 1 + k * high + b)
                 values.append((0.5 * half_width) * twice + centre * v)
             restore(values, send_a, k)
     for c in range(chunks):
         send_out(send_a, applied_ref, 1, c)
     for c in range(chunks):
         wait_out(send_f, filt_ref, 0, c)
+
+    total = filt_ref.shape[1]
+    gram(cell_volume, filt_ref, filt_ref, corr_sum)
+    corr = BlockSum(corr_sum, corr_recv, corr_gath, corr_send, corr_arrive, sum_levels(doms, groups))
+    for step in corr.steps():
+        step()
+    unpack(corr_gath, full)
+
+    for c in range(chunks):
         wait_out(send_a, applied_ref, 1, c)
-
-
-def exchange_filter_call(sent, potential, bounds, groups):
+    gram(cell_volume, filt_ref, applied_ref, hamil_sum)
+    hamil = BlockSum(hamil_sum, hamil_recv, hamil_gath, hamil_send, hamil_arrive, sum_levels(doms, groups))
+    pending = list(hamil.steps())
+    pending.pop(0)()
+
+    def pause():
+        for _ in range(2):
+            if len(pending) > 1:
+                pending.pop(0)()
+
+    calls = [0]
+
+    def sometimes():
+        calls[0] += 1
+        if calls[0] % PAUSE == 0:
+            pause()
+
+    value = inverse_root(full, work, other, sometimes)
+    trans[...] = value
+    turn = split_rounding(value.T)
+
+    bands = out_ref.shape[0]
+    half = total // 2
+    returned = []
+    for part_rows in range(2):
+        for x in range(slab):
+            points = filt_ref[x]
+            piece = [t[part_rows * half : (part_rows + 1) * half] for t in turn]
+            product = dot(piece[0], points) + dot(piece[1], points)
+            for n in range(lanes // LANES):
+                spread[n, pl.ds(x, half, stride=slab), :] = product[:, n * LANES : (n + 1) * LANES]
+        for n in range(lanes // LANES):
+            turned[pl.ds(part_rows * half, half), :, pl.ds(n * LANES, LANES)] = (
+                spread[n].reshape(half, slab, LANES).astype(jnp.bfloat16)
+            )
+        place = out_ref.at[:, :, pl.ds(pl.multiple_of(band * lanes, LANES), lanes)]
+        for q in range(groups // 2):
+            to = part_rows * (groups // 2) + q
+            source = turned.at[pl.ds(to * bands, bands)]
+            returned.append((to, source, place))
+
+            @pl.when(band == to)
+            def _():
+                pltpu.make_async_copy(source, place, back_recv.at[band]).start()
+
+            @pl.when(band != to)
+            def _():
+                remote(source, place, back_send.at[to], back_recv.at[band], {"band": to}).start()
+
+    while pending:
+        pending.pop(0)()
+    unpack(hamil_gath, full)
+    transposed = split_rounding(trans[...].T)
+    halfway = split_rounding(dot3(transposed, split_rounding(full[...])))
+    proj_ref[...] = dot3(halfway, split_rounding(trans[...]))
+
+    for to, source, place in returned:
+        theirs = out_ref.at[:, :, pl.ds(to * lanes, lanes)]
+
+        @pl.when(band == to)
+        def _():
+            pltpu.make_async_copy(source, place, back_recv.at[band]).wait()
+
+        @pl.when(band != to)
+        def _():
+            remote(source, place, back_send.at[to], back_recv.at[band], {"band": to}).wait_send()
+            remote(source, theirs, back_send.at[to], back_recv.at[to], {"band": to}).wait_recv()
+
+
+def step_call(sent, potential, bounds, groups, cell_volume):
     doms, slab, mine, width = sent.shape
     devices = doms * groups
+    total = devices * mine
     planes = doms * slab
     part = min(mine, 8)
     chunks = mine // part
     levels = width // LANES
     lanes = width // groups
     size = LANES * (LANES // GRID_Z)
-    out = jax.ShapeDtypeStruct((slab, devices * mine, lanes), jnp.bfloat16)
+    packed = LANES * len(upper_blocks(total))
     vmem = pl.BlockSpec(memory_space=pltpu.VMEM)
     hbm = pl.BlockSpec(memory_space=pl.ANY)
+    gathered = pltpu.VMEM((slab, total, lanes), jnp.bfloat16)
     whole = pltpu.VMEM((planes, mine, width), jnp.bfloat16)
     order = pltpu.VMEM((size, size), jnp.bfloat16)
+    field = pltpu.VMEM((levels + 2, planes * part, LANES), jnp.float32)
+    triangle = pltpu.VMEM((packed, LANES), jnp.float32)
+    square = pltpu.VMEM((total, total), jnp.float32)
     dma = pltpu.SemaphoreType.DMA
+    most = max(2, doms, groups // 2)
     return pl.pallas_call(
-        functools.partial(exchange_filter, groups),
-        out_shape=(out, out),
+        functools.partial(step_kernel, groups, cell_volume),
+        out_shape=(
+            jax.ShapeDtypeStruct((mine * doms, slab, width), jnp.bfloat16),
+            jax.ShapeDtypeStruct((total, total), jnp.float32),
+        ),
         in_specs=[pl.BlockSpec(memory_space=pltpu.SMEM), hbm, vmem],
-        out_specs=(vmem, vmem),
+        out_specs=(hbm, vmem),
         scratch_shapes=[
+            gathered,
+            gathered,
             pltpu.VMEM(sent.shape, jnp.bfloat16),
             pltpu.VMEM((doms, slab, width), jnp.float32),
             order,
             order,
-            pltpu.VMEM((2, levels + 2, planes * part, LANES), jnp.float32),
+            field,
+            field,
             pltpu.VMEM((levels, planes * part, LANES), jnp.float32),
             whole,
             whole,
+        ]
+        + [triangle] * 6
+        + [square] * 4
+        + [
+            pltpu.VMEM((lanes // LANES, total // 2 * slab, LANES), jnp.float32),
+            pltpu.VMEM((total, slab, lanes), jnp.bfloat16),
             dma((chunks, doms)),
             dma((chunks, doms)),
             dma((doms,)),
             dma((doms,)),
             dma((2, chunks, devices)),
             dma((2, chunks, devices)),
-        ],
-        compiler_params=pltpu.CompilerParams(vmem_limit_bytes=40 << 20, collective_id=2, has_side_effects=True),
+        ]
+        + [dma((2, 3, most))] * 4
+        + [dma((groups,))] * 2,
+        cost_estimate=pl.CostEstimate(flops=60 * total**3, bytes_accessed=8 << 20, transcendentals=0),
+        compiler_params=pltpu.CompilerParams(vmem_limit_bytes=48 << 20, collective_id=2, has_side_effects=True),
     )(bounds, sent, potential)
 
 
@@ -612,37 +858,13 @@
     doms = lax.axis_size("dom")
     groups = lax.axis_size("band")
     mine = bands // doms
-    if mine % 8 or width % (groups * LANES):
+    total = bands * groups
+    blocks = len(upper_blocks(total))
+    if mine % 8 or width % (groups * LANES) or total % (2 * LANES) or blocks * LANES % (8 * doms * groups):
         return body_plain(orbitals, potential, bounds)
-    total_bands = bands * groups
     cell_volume = 1.0 / (slab * doms * width)
     sent = orbitals.reshape(doms, mine, slab, width).transpose(0, 2, 1, 3)
-    filt, applied = exchange_filter_call(sent, potential, bounds, groups)
-    filt = filt.transpose(1, 0, 2).reshape(total_bands, -1)
-    applied = applied.transpose(1, 0, 2).reshape(total_bands, -1)
-    bits = exchange_bits(doms, groups)
-    square = jax.ShapeDtypeStruct((total_bands, total_bands), jnp.float32)
-    rotated, trans = sum_call(
-        functools.partial(orthonormal_kernel, bits, cell_volume, (1, 1, total_bands)),
-        (filt,),
-        (jax.ShapeDtypeStruct(filt.shape, jnp.bfloat16), square),
-        3,
-        bits,
-        0,
-        40 * total_bands**3,
-    )
-    out = lax.all_to_all(rotated, "band", split_axis=0, concat_axis=1, tiled=True)
-    out = out.reshape(bands, groups, slab, width // groups).transpose(0, 2, 1, 3)
-    projected = sum_call(
-        functools.partial(project_kernel, bits, cell_volume),
-        (filt, applied, trans),
-        square,
-        0,
-        bits,
-        1,
-        40 * total_bands**3,
-    )
-    return out.reshape(bands, slab, width), projected
+    return step_call(sent, potential, bounds, groups, cell_volume)
 
 
 def solution(mesh):

time: 205 us -> 144 us (0.70)
  Pallas kernels: 189 us -> 138 us
  starting transfers between devices: 5.43 us -> 0 us
  local copies, waits for them, and re-layouts: 8.24 us -> 4.4 us
    pallas_call x3 -> x1, Pallas kernels: 189 us -> 138 us  [step_call(): pl.pallas_call(functools.partial(step_kernel, groups, cell_volume), out_s...]
    all_to_all x1 -> x0, starting transfers between devices: 5.43 us -> none  [body(): lax.all_to_all(rotated, 'band', split_axis=0, concat_axis=1, tiled=True)]
    reshape x5 -> x0, local copies, waits for them, and re-layouts: 4.81 us -> none  [the longest x2 2.98 us: body(): out.reshape(bands, groups, slab, width // groups).transpose(0, 2, 1, 3)]
  transfers between devices with their start and end apart: 1 -> 0, of which waited for: 0 -> 0; matrix products, arithmetic and copies ran while one was open for 0% -> 0% of each run, Pallas kernels for 24% -> 0%
where the time goes in v2:
time: 144 us; the launch traced here: 143 us
  Pallas kernels  138 us (96%)
  local copies, waits for them, and re-layouts  4.4 us (3%)
    pallas_call x1, Pallas kernels, step_call(): pl.pallas_call(functools.partial(step_kernel, groups, cell_volume), out_s...  138 us

profile of v2, /device:TPU:10, one launch (start us, length us, event | category | flops | bytes accessed | tf_op | source)
XLA Modules:
  0.0 143.2 jit_solution(15983274846387904552)
XLA Ops:
  0.6 0.0 copy-start
  0.6 1.8 %copy.10 = bf16[4,16,4,2048]{3,1,2,0:T(8,128)(2,1)S(1)} copy(bf16[4,16,4,2048]{3,2,1,0:T(4,128)(2,1)} %bitcast.5) | data formatting | bytes 2097152 | tf_op jit(solution)/shard_map/reshape | solution.py:866
  2.5 0.0 copy-start.1
  2.5 0.0 copy-done
  2.5 0.6 copy-done.1
  3.1 138.1 %shard_map.50 = (bf16[64,4,2048]{2,1,0:T(4,128)(2,1)S(1)}, f32[512,512]{1,0:T(8,128)S(1)}) custom-call(f32[2]{0:T(128)S(1)} %copy-done.1, bf16[4,4,16,2048]{3,2,1,0:T(8,128)(2,1)S(1)} %bitcast.4, f32[4,2048]{1,0:T(4,128)S(1)} %copy-done), custom_call_target="tpu_custom_call" | custom-call | flops 8053063680 | bytes 8388608 | tf_op jit(solution)/shard_map/pallas_call | solution.py:769
  141.2 1.0 copy.13
  142.2 1.0 copy.14
Async XLA Ops:
  0.6 1.8 %copy-start = (f32[4,2048]{1,0:T(4,128)S(1)}, f32[4,2048]{1,0:T(4,128)}, u32[]{:S(2)}) copy-start(f32[4,2048]{1,0:T(4,128)} %pot_ref.1) | copy-start | bytes 98308
  2.5 0.7 copy-start.1

commit v3 on v2

--- a/solution.py
+++ b/solution.py
@@ -12,7 +12,7 @@
 NS_STEPS = 8
 LANES = 128
 UNROLL = 8
-PAUSE = 2
+PAUSE = 3
 TILE_ROWS = 8
 
 
@@ -328,7 +328,7 @@
     barrier = pltpu.get_barrier_semaphore()
     for other in others:
         pl.semaphore_signal(barrier, inc=1, device_id=other, device_id_type=pl.DeviceIdType.MESH)
-    pl.semaphore_wait(barrier, len(others))
+    return barrier
 
 
 def lane_orders(perm, back):
@@ -425,21 +425,30 @@
     return [(i, j) for i in range(count) for j in range(i, count)]
 
 
-def gram(cell_volume, left, right, packed):
-    slab, total, _ = left.shape
+def next_cells(nexts):
+    size = nexts.shape[0]
+    row = lax.broadcasted_iota(jnp.int32, (size, size), 0)
+    col = lax.broadcasted_iota(jnp.int32, (size, size), 1)
+    ahead = col // GRID_Z * GRID_Z + lax.rem(col + 1, GRID_Z)
+    nexts[...] = jnp.where((row == ahead) | (row == col + GRID_Z), 1.0, 0.0).astype(jnp.bfloat16)
+
+
+def gram(factor, pairs, slab, packed):
+    total = pairs[0][0].shape[1]
     size = 2 * LANES
     where = {pair: n for n, pair in enumerate(upper_blocks(total))}
     for i in range(total // size):
         for j in range(i, total // size):
             block = jnp.zeros((size, size), jnp.float32)
             for x in range(slab):
-                block = block + lax.dot_general(
-                    left[x, pl.ds(i * size, size), :],
-                    right[x, pl.ds(j * size, size), :],
-                    (((1,), (1,)), ((), ())),
-                    preferred_element_type=jnp.float32,
-                )
-            block = block * cell_volume
+                for left, right in pairs:
+                    block = block + lax.dot_general(
+                        left[x, pl.ds(i * size, size), :],
+                        right[x, pl.ds(j * size, size), :],
+                        (((1,), (1,)), ((), ())),
+                        preferred_element_type=jnp.float32,
+                    )
+            block = block * factor
             for a in range(2):
                 for b in range(2):
                     pair = (2 * i + a, 2 * j + b)
@@ -503,7 +512,7 @@
 
 def step_kernel(
     groups, cell_volume, bounds_ref, sent_ref, pot_ref, out_ref, proj_ref,
-    filt_ref, applied_ref, stage, pots, perm, back, even, odd, diag, send_f, send_a,
+    filt_ref, beyond, image_ref, nexts, stage, pots, perm, back, even, odd, diag, send_f, send_y,
     corr_sum, corr_recv, corr_gath, hamil_sum, hamil_recv, hamil_gath, full, work, other, trans, spread, turned,
     in_send, in_recv, pot_send, pot_recv, out_send, out_recv, corr_send, corr_arrive, hamil_send, hamil_arrive, back_send, back_recv,
 ):
@@ -524,7 +533,9 @@
     inv_half = 1.0 / half_width
 
     everyone = peers(doms, groups)
-    greet(everyone[1:])
+    barrier = greet(everyone[1:])
+    lane_orders(perm, back)
+    pl.semaphore_wait(barrier, len(everyone) - 1)
 
     def incoming(c, r):
         peer = lax.rem(dom + r, doms)
@@ -545,8 +556,8 @@
         for r in range(doms):
             incoming(c, r).start()
 
-    lane_orders(perm, back)
     lane = lax.broadcasted_iota(jnp.int32, (rows, LANES), 1)
+    row_of_lane = lax.broadcasted_iota(jnp.int32, (doms, part, LANES), 2) // GRID_Z
     first_high = lax.rem(lane, high) == 0
     last_high = lax.rem(lane, high) == high - 1
 
@@ -592,30 +603,24 @@
         lax.fori_loop(0, levels // UNROLL, run, 0)
         edges(target)
 
-    def outgoing(source, target, which, c):
+    def outgoing(c):
         copies = []
         row = pl.multiple_of((band * doms + dom) * mine + c * part, part)
-        place = target.at[:, pl.ds(row, part), :]
+        some = pl.ds(c * part, part)
         for r, device in enumerate(everyone):
-            piece = source.at[
-                pl.ds(device["dom"] * slab, slab),
-                pl.ds(c * part, part),
-                pl.ds(pl.multiple_of(device["band"] * lanes, LANES), lanes),
-            ]
-            recv = out_recv.at[which, c, r]
-            if r == 0:
-                copies.append(pltpu.make_async_copy(piece, place, recv))
-            else:
-                copies.append(remote(piece, place, out_send.at[which, c, r], recv, device))
+            here = pl.ds(pl.multiple_of(device["band"] * lanes, LANES), lanes)
+            above = pl.ds(pl.multiple_of(lax.rem(device["band"] + 1, groups) * LANES, LANES), LANES)
+            pairs = (
+                (send_f.at[pl.ds(device["dom"] * slab, slab + 1), some, here], filt_ref.at[:, pl.ds(row, part), :]),
+                (send_y.at[device["dom"], some, above], beyond.at[pl.ds(row, part), :]),
+            )
+            for which, (piece, place) in enumerate(pairs):
+                recv = out_recv.at[which, c, r]
+                if r == 0:
+                    copies.append(pltpu.make_async_copy(piece, place, recv))
+                else:
+                    copies.append(remote(piece, place, out_send.at[which, c, r], recv, device))
         return copies
-
-    def send_out(source, target, which, c):
-        for copy in outgoing(source, target, which, c):
-            copy.start()
-
-    def wait_out(source, target, which, c):
-        for copy in outgoing(source, target, which, c):
-            copy.wait()
 
     for c in range(chunks):
         for r in range(doms):
@@ -646,37 +651,52 @@
             sweep(odd, even, False)
             last = even
 
-        def restore(values, target, k):
+        for k in range(spans):
+            values = [last[1 + k * high + b] for b in range(high)]
             natural = dot(jnp.concatenate(values, axis=1).astype(jnp.bfloat16), back[...])
             for h in range(high):
-                target[:, some, pl.ds((h * spans + k) * LANES, LANES)] = (
-                    natural[:, h * LANES : (h + 1) * LANES].reshape(planes, part, LANES).astype(jnp.bfloat16)
-                )
-
-        for k in range(spans):
-            restore([last[1 + k * high + b] for b in range(high)], send_f, k)
-        send_out(send_f, filt_ref, 0, c)
-        for k in range(spans):
-            values = []
-            for b in range(high):
-                twice, v = image(last, 1 + k * high + b)
-                values.append((0.5 * half_width) * twice + centre * v)
-            restore(values, send_a, k)
+                column = (h * spans + k) * LANES
+                value = natural[:, h * LANES : (h + 1) * LANES].reshape(planes, part, LANES)
+                send_f[pl.ds(0, planes), some, pl.ds(column, LANES)] = value.astype(jnp.bfloat16)
+                send_f[planes, some, pl.ds(column, LANES)] = value[0].astype(jnp.bfloat16)
+                if column % lanes == 0:
+                    value = value.reshape(doms, slab * part, LANES)
+                    edge = value[:, :part]
+                    for x in range(1, slab):
+                        moved = value[:, x * part : (x + 1) * part].reshape(doms * part, LANES)
+                        moved = pltpu.roll(moved, x * GRID_Z, 1).reshape(doms, part, LANES)
+                        edge = jnp.where(row_of_lane == x, moved, edge)
+                    send_y[:, some, pl.ds(column // lanes * LANES, LANES)] = edge.astype(jnp.bfloat16)
+        for copy in outgoing(c):
+            copy.start()
+    next_cells(nexts)
     for c in range(chunks):
-        send_out(send_a, applied_ref, 1, c)
-    for c in range(chunks):
-        wait_out(send_f, filt_ref, 0, c)
+        for copy in outgoing(c):
+            copy.wait()
 
     total = filt_ref.shape[1]
-    gram(cell_volume, filt_ref, filt_ref, corr_sum)
+    gram(cell_volume, ((filt_ref, filt_ref),), slab, corr_sum)
     corr = BlockSum(corr_sum, corr_recv, corr_gath, corr_send, corr_arrive, sum_levels(doms, groups))
-    for step in corr.steps():
+    steps = list(corr.steps())
+    for step in steps[:1]:
+        step()
+    edge = lax.broadcasted_iota(jnp.int32, (total, LANES), 1) >= LANES - GRID_Z
+    for x in range(slab):
+        pot = 3.0 + pot_ref[pl.ds(x, 1), pl.ds(pl.multiple_of(band * lanes, LANES), lanes)]
+        value = filt_ref[x].astype(jnp.float32) * pot - filt_ref[x + 1].astype(jnp.float32)
+        value = value - dot(filt_ref[x], nexts[...])
+        after = pltpu.roll(beyond[...].astype(jnp.float32), (LANES - GRID_Z - x * GRID_Z) % LANES, 1)
+        image_ref[x, :, pl.ds(0, lanes - LANES)] = value[:, : lanes - LANES].astype(jnp.bfloat16)
+        image_ref[x, :, pl.ds(lanes - LANES, LANES)] = (
+            value[:, lanes - LANES :] - jnp.where(edge, after, 0.0)
+        ).astype(jnp.bfloat16)
+    for step in steps[1:3]:
+        step()
+    gram(0.5 * cell_volume, ((filt_ref, image_ref), (image_ref, filt_ref)), slab, hamil_sum)
+    for step in steps[3:]:
         step()
     unpack(corr_gath, full)
 
-    for c in range(chunks):
-        wait_out(send_a, applied_ref, 1, c)
-    gram(cell_volume, filt_ref, applied_ref, hamil_sum)
     hamil = BlockSum(hamil_sum, hamil_recv, hamil_gath, hamil_send, hamil_arrive, sum_levels(doms, groups))
     pending = list(hamil.steps())
     pending.pop(0)()
@@ -695,7 +715,7 @@
 
     value = inverse_root(full, work, other, sometimes)
     trans[...] = value
-    turn = split_rounding(value.T)
+    turn = split(value.T)
 
     bands = out_ref.shape[0]
     half = total // 2
@@ -758,8 +778,6 @@
     packed = LANES * len(upper_blocks(total))
     vmem = pl.BlockSpec(memory_space=pltpu.VMEM)
     hbm = pl.BlockSpec(memory_space=pl.ANY)
-    gathered = pltpu.VMEM((slab, total, lanes), jnp.bfloat16)
-    whole = pltpu.VMEM((planes, mine, width), jnp.bfloat16)
     order = pltpu.VMEM((size, size), jnp.bfloat16)
     field = pltpu.VMEM((levels + 2, planes * part, LANES), jnp.float32)
     triangle = pltpu.VMEM((packed, LANES), jnp.float32)
@@ -775,8 +793,10 @@
         in_specs=[pl.BlockSpec(memory_space=pltpu.SMEM), hbm, vmem],
         out_specs=(hbm, vmem),
         scratch_shapes=[
-            gathered,
-            gathered,
+            pltpu.VMEM((slab + 1, total, lanes), jnp.bfloat16),
+            pltpu.VMEM((total, LANES), jnp.bfloat16),
+            pltpu.VMEM((slab, total, lanes), jnp.bfloat16),
+            pltpu.VMEM((lanes, lanes), jnp.bfloat16),
             pltpu.VMEM(sent.shape, jnp.bfloat16),
             pltpu.VMEM((doms, slab, width), jnp.float32),
             order,
@@ -784,8 +804,8 @@
             field,
             field,
             pltpu.VMEM((levels, planes * part, LANES), jnp.float32),
-            whole,
-            whole,
+            pltpu.VMEM((planes + 1, mine, width), jnp.bfloat16),
+            pltpu.VMEM((doms, mine, groups * LANES), jnp.bfloat16),
         ]
         + [triangle] * 6
         + [square] * 4
@@ -860,7 +880,7 @@
     mine = bands // doms
     total = bands * groups
     blocks = len(upper_blocks(total))
-    if mine % 8 or width % (groups * LANES) or total % (2 * LANES) or blocks * LANES % (8 * doms * groups):
+    if mine % 8 or slab * GRID_Z != LANES or width % (groups * LANES) or total % (2 * LANES) or blocks * LANES % (8 * doms * groups):
         return body_plain(orbitals, potential, bounds)
     cell_volume = 1.0 / (slab * doms * width)
     sent = orbitals.reshape(doms, mine, slab, width).transpose(0, 2, 1, 3)

time: 144 us -> 143 us (level)
  no operation moved by 1% of the time
where the time goes in v3:
time: 143 us
  Pallas kernels  138 us (97%)
  local copies, waits for them, and re-layouts  4.4 us (3%)
    pallas_call x1, Pallas kernels, step_call(): pl.pallas_call(functools.partial(step_kernel, groups, cell_volume), out_s...  138 us

profile of v3, /device:TPU:10, one launch (start us, length us, event | category | flops | bytes accessed | tf_op | source)
XLA Modules:
  0.0 142.6 jit_solution(5501113456124416101)
XLA Ops:
  0.6 0.0 copy-start
  0.6 1.8 %copy.10 = bf16[4,16,4,2048]{3,1,2,0:T(8,128)(2,1)S(1)} copy(bf16[4,16,4,2048]{3,2,1,0:T(4,128)(2,1)} %bitcast.5) | data formatting | bytes 2097152 | tf_op jit(solution)/shard_map/reshape | solution.py:886
  2.5 0.0 copy-start.1
  2.5 0.0 copy-done
  2.5 0.6 copy-done.1
  3.1 137.6 %shard_map.50 = (bf16[64,4,2048]{2,1,0:T(4,128)(2,1)S(1)}, f32[512,512]{1,0:T(8,128)S(1)}) custom-call(f32[2]{0:T(128)S(1)} %copy-done.1, bf16[4,4,16,2048]{3,2,1,0:T(8,128)(2,1)S(1)} %bitcast.4, f32[4,2048]{1,0:T(4,128)S(1)} %copy-done), custom_call_target="tpu_custom_call" | custom-call | flops 8053063680 | bytes 8388608 | tf_op jit(solution)/shard_map/pallas_call | solution.py:787
  140.7 1.0 copy.13
  141.6 1.0 copy.14
Async XLA Ops:
  0.6 1.8 %copy-start = (f32[4,2048]{1,0:T(4,128)S(1)}, f32[4,2048]{1,0:T(4,128)}, u32[]{:S(2)}) copy-start(f32[4,2048]{1,0:T(4,128)} %pot_ref.1) | copy-start | bytes 98308
  2.5 0.7 copy-start.1

commit v4 on v3

--- a/solution.py
+++ b/solution.py
@@ -433,29 +433,25 @@
     nexts[...] = jnp.where((row == ahead) | (row == col + GRID_Z), 1.0, 0.0).astype(jnp.bfloat16)
 
 
-def gram(factor, pairs, slab, packed):
-    total = pairs[0][0].shape[1]
+def gram(factor, left, flipped, packed, halve):
+    slab, lanes, total = flipped.shape
     size = 2 * LANES
-    where = {pair: n for n, pair in enumerate(upper_blocks(total))}
-    for i in range(total // size):
-        for j in range(i, total // size):
-            block = jnp.zeros((size, size), jnp.float32)
-            for x in range(slab):
-                for left, right in pairs:
-                    block = block + lax.dot_general(
-                        left[x, pl.ds(i * size, size), :],
-                        right[x, pl.ds(j * size, size), :],
-                        (((1,), (1,)), ((), ())),
-                        preferred_element_type=jnp.float32,
-                    )
-            block = block * factor
-            for a in range(2):
-                for b in range(2):
-                    pair = (2 * i + a, 2 * j + b)
-                    if pair in where:
-                        packed[pl.ds(where[pair] * LANES, LANES)] = block[
-                            a * LANES : (a + 1) * LANES, b * LANES : (b + 1) * LANES
-                        ]
+    count = total // size
+    product = {}
+    for i in range(count):
+        first = 0 if halve else i * size
+        block = jnp.zeros((size, total - first), jnp.float32)
+        for x in range(slab):
+            block = block + dot(left[x, pl.ds(i * size, size), :], flipped[x, :, pl.ds(first, total - first)])
+        for a in range(2):
+            for j in range(first // LANES, total // LANES):
+                column = j * LANES - first
+                product[2 * i + a, j] = block[a * LANES : (a + 1) * LANES, column : column + LANES]
+    for n, (i, j) in enumerate(upper_blocks(total)):
+        value = product[i, j]
+        if halve:
+            value = 0.5 * (value + product[j, i].T)
+        packed[pl.ds(n * LANES, LANES)] = value * factor
 
 
 def unpack(packed, full):
@@ -466,11 +462,6 @@
             full[pl.ds(j * LANES, LANES), pl.ds(i * LANES, LANES)] = block.T
 
 
-def split_rounding(value):
-    high = value.astype(jnp.bfloat16)
-    return high, (value - high.astype(jnp.float32)).astype(jnp.bfloat16)
-
-
 def inverse_root(full, work, other, pause):
     size = full.shape[0]
     row = lax.broadcasted_iota(jnp.int32, (size, size), 0)
@@ -483,21 +474,21 @@
     scale = jnp.sqrt(jnp.sum(corr * corr) + 1e-06)
     work[...] = corr / scale
     for double in range(NS_STEPS // 2 - 1):
-        held = split_rounding(work[...])
+        held = split(work[...])
         other[...] = dot3(held, held)
         pause()
         square = other[...]
-        rest = dot3(split_rounding(square), split_rounding(0.0625 * square - 0.5625 * work[...]))
-        factor = split_rounding(diagonal(2.25) - 2.4375 * work[...] + (1.6875 * square + rest))
+        rest = dot3(split(square), split(0.0625 * square - 0.5625 * work[...]))
+        factor = split(diagonal(2.25) - 2.4375 * work[...] + (1.6875 * square + rest))
         pause()
         if double == 0:
             full[...] = factor[0].astype(jnp.float32) + factor[1].astype(jnp.float32)
         else:
-            full[...] = dot3(split_rounding(full[...]), factor)
+            full[...] = dot3(split(full[...]), factor)
             pause()
         other[...] = dot3(held, factor)
         pause()
-        work[...] = dot3(split_rounding(other[...]), factor)
+        work[...] = dot3(split(other[...]), factor)
         pause()
     left = diagonal(1.0) - work[...]
     rounded = left.astype(jnp.bfloat16)
@@ -512,7 +503,7 @@
 
 def step_kernel(
     groups, cell_volume, bounds_ref, sent_ref, pot_ref, out_ref, proj_ref,
-    filt_ref, beyond, image_ref, nexts, stage, pots, perm, back, even, odd, diag, send_f, send_y,
+    filt_ref, beyond, image_ref, flipped, nexts, stage, pots, perm, back, even, odd, diag, send_f, send_y,
     corr_sum, corr_recv, corr_gath, hamil_sum, hamil_recv, hamil_gath, full, work, other, trans, spread, turned,
     in_send, in_recv, pot_send, pot_recv, out_send, out_recv, corr_send, corr_arrive, hamil_send, hamil_arrive, back_send, back_recv,
 ):
@@ -603,24 +594,33 @@
         lax.fori_loop(0, levels // UNROLL, run, 0)
         edges(target)
 
-    def outgoing(c):
+    first_row = pl.multiple_of((band * doms + dom) * mine, part)
+
+    def outgoing(pieces):
         copies = []
-        row = pl.multiple_of((band * doms + dom) * mine + c * part, part)
-        some = pl.ds(c * part, part)
         for r, device in enumerate(everyone):
-            here = pl.ds(pl.multiple_of(device["band"] * lanes, LANES), lanes)
-            above = pl.ds(pl.multiple_of(lax.rem(device["band"] + 1, groups) * LANES, LANES), LANES)
-            pairs = (
-                (send_f.at[pl.ds(device["dom"] * slab, slab + 1), some, here], filt_ref.at[:, pl.ds(row, part), :]),
-                (send_y.at[device["dom"], some, above], beyond.at[pl.ds(row, part), :]),
-            )
-            for which, (piece, place) in enumerate(pairs):
-                recv = out_recv.at[which, c, r]
+            for which, piece, place in pieces(device):
+                recv = out_recv.at[which, r]
                 if r == 0:
                     copies.append(pltpu.make_async_copy(piece, place, recv))
                 else:
-                    copies.append(remote(piece, place, out_send.at[which, c, r], recv, device))
+                    copies.append(remote(piece, place, out_send.at[which, r], recv, device))
         return copies
+
+    def block(device):
+        return pl.ds(pl.multiple_of(device["band"] * lanes, LANES), lanes)
+
+    def main(c, device):
+        source = send_f.at[pl.ds(device["dom"] * slab, slab), pl.ds(c * part, part), block(device)]
+        return [(c, source, filt_ref.at[pl.ds(0, slab), pl.ds(first_row + c * part, part), :])]
+
+    def halo(device):
+        above = pl.ds(pl.multiple_of(lax.rem(device["band"] + 1, groups) * LANES, LANES), LANES)
+        rows_here = pl.ds(first_row, mine)
+        return [
+            (chunks, send_f.at[device["dom"] * slab + slab, :, block(device)], filt_ref.at[slab, rows_here, :]),
+            (chunks + 1, send_y.at[device["dom"], :, above], beyond.at[rows_here, :]),
+        ]
 
     for c in range(chunks):
         for r in range(doms):
@@ -667,19 +667,24 @@
                         moved = pltpu.roll(moved, x * GRID_Z, 1).reshape(doms, part, LANES)
                         edge = jnp.where(row_of_lane == x, moved, edge)
                     send_y[:, some, pl.ds(column // lanes * LANES, LANES)] = edge.astype(jnp.bfloat16)
-        for copy in outgoing(c):
+        for copy in outgoing(functools.partial(main, c)):
             copy.start()
+    for copy in outgoing(halo):
+        copy.start()
     next_cells(nexts)
     for c in range(chunks):
-        for copy in outgoing(c):
+        for copy in outgoing(functools.partial(main, c)):
             copy.wait()
 
     total = filt_ref.shape[1]
-    gram(cell_volume, ((filt_ref, filt_ref),), slab, corr_sum)
+    for x in range(slab):
+        flipped[x] = filt_ref[x].T
+    gram(cell_volume, filt_ref, flipped, corr_sum, False)
     corr = BlockSum(corr_sum, corr_recv, corr_gath, corr_send, corr_arrive, sum_levels(doms, groups))
     steps = list(corr.steps())
-    for step in steps[:1]:
-        step()
+    steps[0]()
+    for copy in outgoing(halo):
+        copy.wait()
     edge = lax.broadcasted_iota(jnp.int32, (total, LANES), 1) >= LANES - GRID_Z
     for x in range(slab):
         pot = 3.0 + pot_ref[pl.ds(x, 1), pl.ds(pl.multiple_of(band * lanes, LANES), lanes)]
@@ -692,14 +697,19 @@
         ).astype(jnp.bfloat16)
     for step in steps[1:3]:
         step()
-    gram(0.5 * cell_volume, ((filt_ref, image_ref), (image_ref, filt_ref)), slab, hamil_sum)
-    for step in steps[3:]:
-        step()
-    unpack(corr_gath, full)
-
+    gram(cell_volume, image_ref, flipped, hamil_sum, True)
     hamil = BlockSum(hamil_sum, hamil_recv, hamil_gath, hamil_send, hamil_arrive, sum_levels(doms, groups))
     pending = list(hamil.steps())
     pending.pop(0)()
+    steps = steps[3:]
+    while steps:
+        for _ in range(2):
+            if steps:
+                steps.pop(0)()
+        for _ in range(2):
+            if steps:
+                pending.pop(0)()
+    unpack(corr_gath, full)
 
     def pause():
         for _ in range(2):
@@ -748,9 +758,9 @@
     while pending:
         pending.pop(0)()
     unpack(hamil_gath, full)
-    transposed = split_rounding(trans[...].T)
-    halfway = split_rounding(dot3(transposed, split_rounding(full[...])))
-    proj_ref[...] = dot3(halfway, split_rounding(trans[...]))
+    transposed = split(trans[...].T)
+    halfway = split(dot3(transposed, split(full[...])))
+    proj_ref[...] = dot3(halfway, split(trans[...]))
 
     for to, source, place in returned:
         theirs = out_ref.at[:, :, pl.ds(to * lanes, lanes)]
@@ -796,6 +806,7 @@
             pltpu.VMEM((slab + 1, total, lanes), jnp.bfloat16),
             pltpu.VMEM((total, LANES), jnp.bfloat16),
             pltpu.VMEM((slab, total, lanes), jnp.bfloat16),
+            pltpu.VMEM((slab, lanes, total), jnp.bfloat16),
             pltpu.VMEM((lanes, lanes), jnp.bfloat16),
             pltpu.VMEM(sent.shape, jnp.bfloat16),
             pltpu.VMEM((doms, slab, width), jnp.float32),
@@ -816,8 +827,8 @@
             dma((chunks, doms)),
             dma((doms,)),
             dma((doms,)),
-            dma((2, chunks, devices)),
-            dma((2, chunks, devices)),
+            dma((chunks + 2, devices)),
+            dma((chunks + 2, devices)),
         ]
         + [dma((2, 3, most))] * 4
         + [dma((groups,))] * 2,

time: 143 us -> 126 us (0.88)
  Pallas kernels: 138 us -> 120 us
    pallas_call x1, Pallas kernels: 138 us -> 120 us  [step_call(): pl.pallas_call(functools.partial(step_kernel, groups, cell_volume), out_s...]
where the time goes in v4:
time: 126 us; the launch traced here: 125 us
  Pallas kernels  120 us (95%)
  local copies, waits for them, and re-layouts  4.4 us (3%)
    pallas_call x1, Pallas kernels, step_call(): pl.pallas_call(functools.partial(step_kernel, groups, cell_volume), out_s...  120 us
    unnamed x6, local copies, waits for them, and re-layouts  2.59 us

profile of v4, /device:TPU:10, one launch (start us, length us, event | category | flops | bytes accessed | tf_op | source)
XLA Modules:
  0.0 125.4 jit_solution(15180444875312847752)
XLA Ops:
  0.6 0.0 copy-start
  0.6 1.8 %copy.10 = bf16[4,16,4,2048]{3,1,2,0:T(8,128)(2,1)S(1)} copy(bf16[4,16,4,2048]{3,2,1,0:T(4,128)(2,1)} %bitcast.5) | data formatting | bytes 2097152 | tf_op jit(solution)/shard_map/reshape | solution.py:897
  2.5 0.0 copy-start.1
  2.5 0.0 copy-done
  2.5 0.6 copy-done.1
  3.1 120.4 %shard_map.50 = (bf16[64,4,2048]{2,1,0:T(4,128)(2,1)S(1)}, f32[512,512]{1,0:T(8,128)S(1)}) custom-call(f32[2]{0:T(128)S(1)} %copy-done.1, bf16[4,4,16,2048]{3,2,1,0:T(8,128)(2,1)S(1)} %bitcast.4, f32[4,2048]{1,0:T(4,128)S(1)} %copy-done), custom_call_target="tpu_custom_call" | custom-call | flops 8053063680 | bytes 8388608 | tf_op jit(solution)/shard_map/pallas_call | solution.py:797
  123.5 1.0 copy.13
  124.5 1.0 copy.14
Async XLA Ops:
  0.6 1.8 %copy-start = (f32[4,2048]{1,0:T(4,128)S(1)}, f32[4,2048]{1,0:T(4,128)}, u32[]{:S(2)}) copy-start(f32[4,2048]{1,0:T(4,128)} %pot_ref.1) | copy-start | bytes 98308
  2.5 0.7 copy-start.1

commit v5 on v4

--- a/solution.py
+++ b/solution.py
@@ -475,10 +475,8 @@
     work[...] = corr / scale
     for double in range(NS_STEPS // 2 - 1):
         held = split(work[...])
-        other[...] = dot3(held, held)
-        pause()
-        square = other[...]
-        rest = dot3(split(square), split(0.0625 * square - 0.5625 * work[...]))
+        square = dot(held[0], held[0])
+        rest = dot(square.astype(jnp.bfloat16), (0.0625 * square - 0.5625 * work[...]).astype(jnp.bfloat16))
         factor = split(diagonal(2.25) - 2.4375 * work[...] + (1.6875 * square + rest))
         pause()
         if double == 0:
@@ -488,7 +486,7 @@
             pause()
         other[...] = dot3(held, factor)
         pause()
-        work[...] = dot3(split(other[...]), factor)
+        work[...] = dot3(factor, split(other[...]))
         pause()
     left = diagonal(1.0) - work[...]
     rounded = left.astype(jnp.bfloat16)
@@ -504,7 +502,7 @@
 def step_kernel(
     groups, cell_volume, bounds_ref, sent_ref, pot_ref, out_ref, proj_ref,
     filt_ref, beyond, image_ref, flipped, nexts, stage, pots, perm, back, even, odd, diag, send_f, send_y,
-    corr_sum, corr_recv, corr_gath, hamil_sum, hamil_recv, hamil_gath, full, work, other, trans, spread, turned,
+    corr_sum, corr_recv, corr_gath, hamil_sum, hamil_recv, hamil_gath, full, work, other, turn, spread, turned,
     in_send, in_recv, pot_send, pot_recv, out_send, out_recv, corr_send, corr_arrive, hamil_send, hamil_arrive, back_send, back_recv,
 ):
     doms, slab, mine, width = stage.shape
@@ -687,7 +685,7 @@
         copy.wait()
     edge = lax.broadcasted_iota(jnp.int32, (total, LANES), 1) >= LANES - GRID_Z
     for x in range(slab):
-        pot = 3.0 + pot_ref[pl.ds(x, 1), pl.ds(pl.multiple_of(band * lanes, LANES), lanes)]
+        pot = 3.0 + pots[dom, pl.ds(x, 1), pl.ds(pl.multiple_of(band * lanes, LANES), lanes)]
         value = filt_ref[x].astype(jnp.float32) * pot - filt_ref[x + 1].astype(jnp.float32)
         value = value - dot(filt_ref[x], nexts[...])
         after = pltpu.roll(beyond[...].astype(jnp.float32), (LANES - GRID_Z - x * GRID_Z) % LANES, 1)
@@ -724,55 +722,41 @@
             pause()
 
     value = inverse_root(full, work, other, sometimes)
-    trans[...] = value
-    turn = split(value.T)
+    turn[0], turn[1] = split(value)
 
     bands = out_ref.shape[0]
     half = total // 2
+    side = groups // 2
+    place = out_ref.at[:, :, pl.ds(pl.multiple_of(band * lanes, LANES), lanes)]
     returned = []
-    for part_rows in range(2):
+    for n in range(2):
+        which = lax.rem(band // side + 1 + n, 2)
+        rows_here = pl.ds(pl.multiple_of(which * half, half), half)
         for x in range(slab):
             points = filt_ref[x]
-            piece = [t[part_rows * half : (part_rows + 1) * half] for t in turn]
-            product = dot(piece[0], points) + dot(piece[1], points)
-            for n in range(lanes // LANES):
-                spread[n, pl.ds(x, half, stride=slab), :] = product[:, n * LANES : (n + 1) * LANES]
-        for n in range(lanes // LANES):
-            turned[pl.ds(part_rows * half, half), :, pl.ds(n * LANES, LANES)] = (
-                spread[n].reshape(half, slab, LANES).astype(jnp.bfloat16)
-            )
-        place = out_ref.at[:, :, pl.ds(pl.multiple_of(band * lanes, LANES), lanes)]
-        for q in range(groups // 2):
-            to = part_rows * (groups // 2) + q
+            product = dot(turn[0, rows_here, :], points) + dot(turn[1, rows_here, :], points)
+            for t in range(lanes // LANES):
+                spread[t, pl.ds(x, half, stride=slab), :] = product[:, t * LANES : (t + 1) * LANES]
+        for t in range(lanes // LANES):
+            turned[rows_here, :, pl.ds(t * LANES, LANES)] = spread[t].reshape(half, slab, LANES).astype(jnp.bfloat16)
+        for q in range(side):
+            to = which * side + lax.rem(band + q, side)
             source = turned.at[pl.ds(to * bands, bands)]
-            returned.append((to, source, place))
-
-            @pl.when(band == to)
-            def _():
-                pltpu.make_async_copy(source, place, back_recv.at[band]).start()
-
-            @pl.when(band != to)
-            def _():
-                remote(source, place, back_send.at[to], back_recv.at[band], {"band": to}).start()
+            recv = back_recv.at[n * side + q]
+            if n == 1 and q == 0:
+                copy = pltpu.make_async_copy(source, place, recv)
+            else:
+                copy = remote(source, place, back_send.at[n * side + q], recv, {"band": to})
+            copy.start()
+            returned.append(copy)
 
     while pending:
         pending.pop(0)()
     unpack(hamil_gath, full)
-    transposed = split(trans[...].T)
-    halfway = split(dot3(transposed, split(full[...])))
-    proj_ref[...] = dot3(halfway, split(trans[...]))
-
-    for to, source, place in returned:
-        theirs = out_ref.at[:, :, pl.ds(to * lanes, lanes)]
-
-        @pl.when(band == to)
-        def _():
-            pltpu.make_async_copy(source, place, back_recv.at[band]).wait()
-
-        @pl.when(band != to)
-        def _():
-            remote(source, place, back_send.at[to], back_recv.at[band], {"band": to}).wait_send()
-            remote(source, theirs, back_send.at[to], back_recv.at[to], {"band": to}).wait_recv()
+    halfway = split(dot3((turn[0], turn[1]), split(full[...])))
+    proj_ref[...] = dot3(halfway, (turn[0], turn[1]))
+    for copy in returned:
+        copy.wait()
 
 
 def step_call(sent, potential, bounds, groups, cell_volume):
@@ -800,7 +784,7 @@
             jax.ShapeDtypeStruct((mine * doms, slab, width), jnp.bfloat16),
             jax.ShapeDtypeStruct((total, total), jnp.float32),
         ),
-        in_specs=[pl.BlockSpec(memory_space=pltpu.SMEM), hbm, vmem],
+        in_specs=[pl.BlockSpec(memory_space=pltpu.SMEM), hbm, hbm],
         out_specs=(hbm, vmem),
         scratch_shapes=[
             pltpu.VMEM((slab + 1, total, lanes), jnp.bfloat16),
@@ -819,8 +803,9 @@
             pltpu.VMEM((doms, mine, groups * LANES), jnp.bfloat16),
         ]
         + [triangle] * 6
-        + [square] * 4
+        + [square] * 3
         + [
+            pltpu.VMEM((2, total, total), jnp.bfloat16),
             pltpu.VMEM((lanes // LANES, total // 2 * slab, LANES), jnp.float32),
             pltpu.VMEM((total, slab, lanes), jnp.bfloat16),
             dma((chunks, doms)),

time: 126 us -> 126 us (level)
  the two profiles are of different devices: /device:TPU:10 before, /device:TPU:0 now
where the time goes in v5:
time: 126 us
  Pallas kernels  120 us (95%)
  local copies, waits for them, and re-layouts  4.4 us (3%)
    pallas_call x1, Pallas kernels, step_call(): pl.pallas_call(functools.partial(step_kernel, groups, cell_volume), out_s...  120 us
    unnamed x6, local copies, waits for them, and re-layouts  2.59 us

profile of v5, /device:TPU:0, one launch (start us, length us, event | category | flops | bytes accessed | tf_op | source)
XLA Modules:
  0.0 125.5 jit_solution(10847823816403642404)
XLA Ops:
  0.6 0.0 copy-start
  0.6 1.8 %copy.10 = bf16[4,16,4,2048]{3,1,2,0:T(8,128)(2,1)S(1)} copy(bf16[4,16,4,2048]{3,2,1,0:T(4,128)(2,1)} %bitcast.5) | data formatting | bytes 2097152 | tf_op jit(solution)/shard_map/reshape | solution.py:882
  2.5 0.0 copy-start.1
  2.5 0.0 copy-done
  2.5 0.6 copy-done.1
  3.1 120.5 %shard_map.50 = (bf16[64,4,2048]{2,1,0:T(4,128)(2,1)S(1)}, f32[512,512]{1,0:T(8,128)S(1)}) custom-call(f32[2]{0:T(128)S(1)} %copy-done.1, bf16[4,4,16,2048]{3,2,1,0:T(8,128)(2,1)S(1)} %bitcast.4, f32[4,2048]{1,0:T(4,128)S(1)} %copy-done), custom_call_target="tpu_custom_call" | custom-call | flops 8053063680 | bytes 8388608 | tf_op jit(solution)/shard_map/pallas_call | solution.py:781
  123.6 1.0 copy.13
  124.6 1.0 copy.14
Async XLA Ops:
  0.6 1.8 %copy-start = (f32[4,2048]{1,0:T(4,128)S(1)}, f32[4,2048]{1,0:T(4,128)}, u32[]{:S(2)}) copy-start(f32[4,2048]{1,0:T(4,128)} %pot_ref.1) | copy-start | bytes 98308
  2.5 0.7 copy-start.1

commit v6 on v5

--- a/solution.py
+++ b/solution.py
@@ -12,6 +12,7 @@
 NS_STEPS = 8
 LANES = 128
 UNROLL = 8
+SHARE = 2
 PAUSE = 3
 TILE_ROWS = 8
 
@@ -425,6 +426,12 @@
     return [(i, j) for i in range(count) for j in range(i, count)]
 
 
+def next_rings(ring, high):
+    row = lax.rem(lax.broadcasted_iota(jnp.int32, ring.shape, 0), LANES)
+    apart = lax.rem(row - lax.broadcasted_iota(jnp.int32, ring.shape, 1) + LANES, LANES)
+    ring[...] = jnp.where((apart == high) | (apart == LANES - high), 1.0, 0.0).astype(jnp.bfloat16)
+
+
 def next_cells(nexts):
     size = nexts.shape[0]
     row = lax.broadcasted_iota(jnp.int32, (size, size), 0)
@@ -501,7 +508,7 @@
 
 def step_kernel(
     groups, cell_volume, bounds_ref, sent_ref, pot_ref, out_ref, proj_ref,
-    filt_ref, beyond, image_ref, flipped, nexts, stage, pots, perm, back, even, odd, diag, send_f, send_y,
+    filt_ref, beyond, image_ref, flipped, nexts, stage, pots, perm, back, ring, even, odd, diag, send_f, send_y,
     corr_sum, corr_recv, corr_gath, hamil_sum, hamil_recv, hamil_gath, full, work, other, turn, spread, turned,
     in_send, in_recv, pot_send, pot_recv, out_send, out_recv, corr_send, corr_arrive, hamil_send, hamil_arrive, back_send, back_recv,
 ):
@@ -524,6 +531,7 @@
     everyone = peers(doms, groups)
     barrier = greet(everyone[1:])
     lane_orders(perm, back)
+    next_rings(ring, high)
     pl.semaphore_wait(barrier, len(everyone) - 1)
 
     def incoming(c, r):
@@ -572,21 +580,33 @@
         low = field[1]
         field[levels + 1] = jnp.where(last_high, pltpu.roll(low, high - 1, 1), pltpu.roll(low, LANES - 1, 1))
 
-    def image(field, i):
-        v = field[i]
-        around = pltpu.roll(v, high, 1) + pltpu.roll(v, LANES - high, 1)
+    cut = rows // SHARE if SHARE else 0
+
+    def sums_z(values):
+        if not cut:
+            return None
+        top = split(jnp.concatenate([v[:cut] for v in values], axis=0))
+        return dot(jnp.concatenate(top, axis=1), ring[...])
+
+    def image(v, field, i, sums):
+        rest = v[cut:]
+        around = pltpu.roll(rest, high, 1) + pltpu.roll(rest, LANES - high, 1)
+        if cut:
+            around = jnp.concatenate([sums, around], axis=0)
         around = around + (field[i - 1] + field[i + 1])
         around = around + (
             jnp.concatenate([v[part:], v[:part]], axis=0) + jnp.concatenate([v[rows - part :], v[: rows - part]], axis=0)
         )
-        return diag[i - 1] * v - inv_half * around, v
+        return diag[i - 1] * v - inv_half * around
 
     def sweep(source, target, first):
         def run(j, carry):
+            start = 1 + j * UNROLL
+            values = [source[start + i] for i in range(UNROLL)]
+            sums = sums_z(values)
             for i in range(UNROLL):
-                i = 1 + j * UNROLL + i
-                fresh = image(source, i)[0]
-                target[i] = 0.5 * fresh if first else fresh - target[i]
+                fresh = image(values[i], source, start + i, sums[i * cut : (i + 1) * cut] if cut else None)
+                target[start + i] = 0.5 * fresh if first else fresh - target[start + i]
             return carry
 
         lax.fori_loop(0, levels // UNROLL, run, 0)
@@ -725,28 +745,28 @@
     turn[0], turn[1] = split(value)
 
     bands = out_ref.shape[0]
-    half = total // 2
-    side = groups // 2
+    parts = groups // 2
+    size = total // parts
     place = out_ref.at[:, :, pl.ds(pl.multiple_of(band * lanes, LANES), lanes)]
     returned = []
-    for n in range(2):
-        which = lax.rem(band // side + 1 + n, 2)
-        rows_here = pl.ds(pl.multiple_of(which * half, half), half)
+    for n, shift in enumerate(sorted(range(parts), key=lambda r: -min(r, parts - r))):
+        which = lax.rem(band // 2 + shift, parts)
+        rows_here = pl.ds(pl.multiple_of(which * size, size), size)
         for x in range(slab):
             points = filt_ref[x]
             product = dot(turn[0, rows_here, :], points) + dot(turn[1, rows_here, :], points)
             for t in range(lanes // LANES):
-                spread[t, pl.ds(x, half, stride=slab), :] = product[:, t * LANES : (t + 1) * LANES]
+                spread[t, pl.ds(x, size, stride=slab), :] = product[:, t * LANES : (t + 1) * LANES]
         for t in range(lanes // LANES):
-            turned[rows_here, :, pl.ds(t * LANES, LANES)] = spread[t].reshape(half, slab, LANES).astype(jnp.bfloat16)
-        for q in range(side):
-            to = which * side + lax.rem(band + q, side)
+            turned[rows_here, :, pl.ds(t * LANES, LANES)] = spread[t].reshape(size, slab, LANES).astype(jnp.bfloat16)
+        for q in (1, 0):
+            to = which * 2 + lax.rem(band + q, 2)
             source = turned.at[pl.ds(to * bands, bands)]
-            recv = back_recv.at[n * side + q]
-            if n == 1 and q == 0:
+            recv = back_recv.at[n * 2 + q]
+            if shift == 0 and q == 0:
                 copy = pltpu.make_async_copy(source, place, recv)
             else:
-                copy = remote(source, place, back_send.at[n * side + q], recv, {"band": to})
+                copy = remote(source, place, back_send.at[n * 2 + q], recv, {"band": to})
             copy.start()
             returned.append(copy)
 
@@ -796,6 +816,7 @@
             pltpu.VMEM((doms, slab, width), jnp.float32),
             order,
             order,
+            pltpu.VMEM((2 * LANES, LANES), jnp.bfloat16),
             field,
             field,
             pltpu.VMEM((levels, planes * part, LANES), jnp.float32),
@@ -806,7 +827,7 @@
         + [square] * 3
         + [
             pltpu.VMEM((2, total, total), jnp.bfloat16),
-            pltpu.VMEM((lanes // LANES, total // 2 * slab, LANES), jnp.float32),
+            pltpu.VMEM((lanes // LANES, total // (groups // 2) * slab, LANES), jnp.float32),
             pltpu.VMEM((total, slab, lanes), jnp.bfloat16),
             dma((chunks, doms)),
             dma((chunks, doms)),

time: 126 us -> 120 us (0.952)
  the two profiles are of different devices: /device:TPU:0 before, /device:TPU:10 now
where the time goes in v6:
time: 120 us
  Pallas kernels  115 us (96%)
  local copies, waits for them, and re-layouts  4.4 us (4%)
    pallas_call x1, Pallas kernels, step_call(): pl.pallas_call(functools.partial(step_kernel, groups, cell_volume), out_s...  115 us
    unnamed x6, local copies, waits for them, and re-layouts  2.59 us

profile of v6, /device:TPU:10, one launch (start us, length us, event | category | flops | bytes accessed | tf_op | source)
XLA Modules:
  0.0 120.2 jit_solution(16435297930165766862)
XLA Ops:
  0.6 0.0 copy-start
  0.6 1.8 %copy.10 = bf16[4,16,4,2048]{3,1,2,0:T(8,128)(2,1)S(1)} copy(bf16[4,16,4,2048]{3,2,1,0:T(4,128)(2,1)} %bitcast.5) | data formatting | bytes 2097152 | tf_op jit(solution)/shard_map/reshape | solution.py:903
  2.5 0.0 copy-start.1
  2.5 0.0 copy-done
  2.5 0.6 copy-done.1
  3.1 115.1 %shard_map.50 = (bf16[64,4,2048]{2,1,0:T(4,128)(2,1)S(1)}, f32[512,512]{1,0:T(8,128)S(1)}) custom-call(f32[2]{0:T(128)S(1)} %copy-done.1, bf16[4,4,16,2048]{3,2,1,0:T(8,128)(2,1)S(1)} %bitcast.4, f32[4,2048]{1,0:T(4,128)S(1)} %copy-done), custom_call_target="tpu_custom_call" | custom-call | flops 8053063680 | bytes 8388608 | tf_op jit(solution)/shard_map/pallas_call | solution.py:801
  118.3 1.0 copy.13
  119.2 1.0 copy.14
Async XLA Ops:
  0.6 1.8 %copy-start = (f32[4,2048]{1,0:T(4,128)S(1)}, f32[4,2048]{1,0:T(4,128)}, u32[]{:S(2)}) copy-start(f32[4,2048]{1,0:T(4,128)} %pot_ref.1) | copy-start | bytes 98308
  2.5 0.7 copy-start.1

commit v7 on v6

--- a/solution.py
+++ b/solution.py
@@ -13,7 +13,7 @@
 LANES = 128
 UNROLL = 8
 SHARE = 2
-PAUSE = 3
+PAUSE = 1
 TILE_ROWS = 8
 
 
@@ -310,8 +310,9 @@
     dom = lax.axis_index("dom")
     band = lax.axis_index("band")
     rows = [lax.rem(dom + r, doms) for r in range(doms)]
-    columns = [lax.rem(band + r, groups) for r in range(groups)]
-    return [{"dom": d, "band": b} for b in columns for d in rows]
+    columns = [lax.rem(band + r, groups) for r in sorted(range(groups), key=lambda r: -min(r, groups - r))]
+    others = [{"dom": d, "band": b} for b in columns for d in rows if b is not columns[-1] or d is not rows[0]]
+    return [{"dom": dom, "band": band}] + others
 
 
 def remote(source, target, send_sem, recv_sem, device):
@@ -700,7 +701,8 @@
     gram(cell_volume, filt_ref, flipped, corr_sum, False)
     corr = BlockSum(corr_sum, corr_recv, corr_gath, corr_send, corr_arrive, sum_levels(doms, groups))
     steps = list(corr.steps())
-    steps[0]()
+    for step in steps[:3]:
+        step()
     for copy in outgoing(halo):
         copy.wait()
     edge = lax.broadcasted_iota(jnp.int32, (total, LANES), 1) >= LANES - GRID_Z
@@ -713,8 +715,6 @@
         image_ref[x, :, pl.ds(lanes - LANES, LANES)] = (
             value[:, lanes - LANES :] - jnp.where(edge, after, 0.0)
         ).astype(jnp.bfloat16)
-    for step in steps[1:3]:
-        step()
     gram(cell_volume, image_ref, flipped, hamil_sum, True)
     hamil = BlockSum(hamil_sum, hamil_recv, hamil_gath, hamil_send, hamil_arrive, sum_levels(doms, groups))
     pending = list(hamil.steps())

time: 120 us -> 116 us (0.967)
  Pallas kernels: 115 us -> 111 us
    pallas_call x1, Pallas kernels: 115 us -> 111 us  [step_call(): pl.pallas_call(functools.partial(step_kernel, groups, cell_volume), out_s...]
where the time goes in v7:
time: 116 us
  Pallas kernels  111 us (96%)
  local copies, waits for them, and re-layouts  4.4 us (4%)
    pallas_call x1, Pallas kernels, step_call(): pl.pallas_call(functools.partial(step_kernel, groups, cell_volume), out_s...  111 us
    unnamed x6, local copies, waits for them, and re-layouts  2.59 us

profile of v7, /device:TPU:10, one launch (start us, length us, event | category | flops | bytes accessed | tf_op | source)
XLA Modules:
  0.0 116.0 jit_solution(16180431989825508148)
XLA Ops:
  0.6 0.0 copy-start
  0.6 1.8 %copy.10 = bf16[4,16,4,2048]{3,1,2,0:T(8,128)(2,1)S(1)} copy(bf16[4,16,4,2048]{3,2,1,0:T(4,128)(2,1)} %bitcast.5) | data formatting | bytes 2097152 | tf_op jit(solution)/shard_map/reshape | solution.py:903
  2.5 0.0 copy-start.1
  2.5 0.0 copy-done
  2.5 0.6 copy-done.1
  3.1 110.9 %shard_map.50 = (bf16[64,4,2048]{2,1,0:T(4,128)(2,1)S(1)}, f32[512,512]{1,0:T(8,128)S(1)}) custom-call(f32[2]{0:T(128)S(1)} %copy-done.1, bf16[4,4,16,2048]{3,2,1,0:T(8,128)(2,1)S(1)} %bitcast.4, f32[4,2048]{1,0:T(4,128)S(1)} %copy-done), custom_call_target="tpu_custom_call" | custom-call | flops 8053063680 | bytes 8388608 | tf_op jit(solution)/shard_map/pallas_call | solution.py:801
  114.0 1.0 copy.13
  115.0 1.0 copy.14
Async XLA Ops:
  0.6 1.8 %copy-start = (f32[4,2048]{1,0:T(4,128)S(1)}, f32[4,2048]{1,0:T(4,128)}, u32[]{:S(2)}) copy-start(f32[4,2048]{1,0:T(4,128)} %pot_ref.1) | copy-start | bytes 98308
  2.5 0.7 copy-start.1

commit v8 on v7

--- a/solution.py
+++ b/solution.py
@@ -11,7 +11,7 @@
 DEG = 8
 NS_STEPS = 8
 LANES = 128
-UNROLL = 8
+UNROLL = 16
 SHARE = 2
 PAUSE = 1
 TILE_ROWS = 8

time: 116 us -> 115 us (level)
  Pallas kernels: 111 us -> 109 us
    pallas_call x1, Pallas kernels: 111 us -> 109 us  [step_call(): pl.pallas_call(functools.partial(step_kernel, groups, cell_volume), out_s...]
where the time goes in v8:
time: 115 us; the launch traced here: 114 us
  Pallas kernels  109 us (95%)
  local copies, waits for them, and re-layouts  4.4 us (4%)
    pallas_call x1, Pallas kernels, step_call(): pl.pallas_call(functools.partial(step_kernel, groups, cell_volume), out_s...  109 us
    unnamed x6, local copies, waits for them, and re-layouts  2.59 us

profile of v8, /device:TPU:10, one launch (start us, length us, event | category | flops | bytes accessed | tf_op | source)
XLA Modules:
  0.0 114.4 jit_solution(14723283364896437096)
XLA Ops:
  0.6 0.0 copy-start
  0.6 1.8 %copy.10 = bf16[4,16,4,2048]{3,1,2,0:T(8,128)(2,1)S(1)} copy(bf16[4,16,4,2048]{3,2,1,0:T(4,128)(2,1)} %bitcast.5) | data formatting | bytes 2097152 | tf_op jit(solution)/shard_map/reshape | solution.py:903
  2.5 0.0 copy-start.1
  2.5 0.0 copy-done
  2.5 0.6 copy-done.1
  3.1 109.3 %shard_map.50 = (bf16[64,4,2048]{2,1,0:T(4,128)(2,1)S(1)}, f32[512,512]{1,0:T(8,128)S(1)}) custom-call(f32[2]{0:T(128)S(1)} %copy-done.1, bf16[4,4,16,2048]{3,2,1,0:T(8,128)(2,1)S(1)} %bitcast.4, f32[4,2048]{1,0:T(4,128)S(1)} %copy-done), custom_call_target="tpu_custom_call" | custom-call | flops 8053063680 | bytes 8388608 | tf_op jit(solution)/shard_map/pallas_call | solution.py:801
  112.4 1.0 copy.13
  113.4 1.0 copy.14
Async XLA Ops:
  0.6 1.8 %copy-start = (f32[4,2048]{1,0:T(4,128)S(1)}, f32[4,2048]{1,0:T(4,128)}, u32[]{:S(2)}) copy-start(f32[4,2048]{1,0:T(4,128)} %pot_ref.1) | copy-start | bytes 98308
  2.5 0.7 copy-start.1

commit v9 on v8

--- a/solution.py
+++ b/solution.py
@@ -12,7 +12,7 @@
 NS_STEPS = 8
 LANES = 128
 UNROLL = 16
-SHARE = 2
+SHARE = 5
 PAUSE = 1
 TILE_ROWS = 8
 
@@ -581,7 +581,7 @@
         low = field[1]
         field[levels + 1] = jnp.where(last_high, pltpu.roll(low, high - 1, 1), pltpu.roll(low, LANES - 1, 1))
 
-    cut = rows // SHARE if SHARE else 0
+    cut = rows * SHARE // 8
 
     def sums_z(values):
         if not cut:

time: 115 us -> 115 us (level)
  no operation moved by 1% of the time
where the time goes in v9:
time: 115 us
  Pallas kernels  109 us (95%)
  local copies, waits for them, and re-layouts  4.4 us (4%)
    pallas_call x1, Pallas kernels, step_call(): pl.pallas_call(functools.partial(step_kernel, groups, cell_volume), out_s...  109 us
    unnamed x6, local copies, waits for them, and re-layouts  2.59 us

profile of v9, /device:TPU:10, one launch (start us, length us, event | category | flops | bytes accessed | tf_op | source)
XLA Modules:
  0.0 114.5 jit_solution(15826880114685206676)
XLA Ops:
  0.6 0.0 copy-start
  0.6 1.8 %copy.10 = bf16[4,16,4,2048]{3,1,2,0:T(8,128)(2,1)S(1)} copy(bf16[4,16,4,2048]{3,2,1,0:T(4,128)(2,1)} %bitcast.5) | data formatting | bytes 2097152 | tf_op jit(solution)/shard_map/reshape | solution.py:903
  2.5 0.0 copy-start.1
  2.5 0.0 copy-done
  2.5 0.6 copy-done.1
  3.1 109.4 %shard_map.50 = (bf16[64,4,2048]{2,1,0:T(4,128)(2,1)S(1)}, f32[512,512]{1,0:T(8,128)S(1)}) custom-call(f32[2]{0:T(128)S(1)} %copy-done.1, bf16[4,4,16,2048]{3,2,1,0:T(8,128)(2,1)S(1)} %bitcast.4, f32[4,2048]{1,0:T(4,128)S(1)} %copy-done), custom_call_target="tpu_custom_call" | custom-call | flops 8053063680 | bytes 8388608 | tf_op jit(solution)/shard_map/pallas_call | solution.py:801
  112.6 1.0 copy.13
  113.5 1.0 copy.14
Async XLA Ops:
  0.6 1.8 %copy-start = (f32[4,2048]{1,0:T(4,128)S(1)}, f32[4,2048]{1,0:T(4,128)}, u32[]{:S(2)}) copy-start(f32[4,2048]{1,0:T(4,128)} %pot_ref.1) | copy-start | bytes 98308
  2.5 0.7 copy-start.1
